TPU v7x, 256 devices: a whole 4x4x8 slice. The times are simulated.
256 devices in a mesh: row: 64 (over z, y, core), col: 4 (over x).
Axes of the slice: x: 4, y: 4, z: 8, core: 2. Of those that a mesh axis runs over, the one named last changes fastest.
Arguments:
- sigma_anc: float32 [8192, 8192], P('row', 'col'), may hold values from -24 to 80, as said below
- panel_hat: float32 [8192, 4096], P('row', 'col'), may hold values from -0.0625 to 0.0625
- pattern: int32 [64, 64], replicated, may hold values from 0 to 1, as said below
- diag_inverse: float32 [4096], P('col'), may hold values from 0.5 to 4
Outputs:
- sigma_cross: float32 [8192, 4096], P('row', 'col')
- variance: float32 [4096], P('col')
Inputs may be any that keep to these rules, and one draw needn't show every extreme that they name: `pattern`: symmetric; every diagonal block is 1. `sigma_anc`: symmetric.
All inputs are finite; a program needn't handle non-finite values.
Results may differ from a plain program's by a relative error of at most 0.000073.
Values sent between devices are 32-bit elements; how exact they have to be, the bound alone decides.
A program may use at most 128 MiB of HBM per device.

v0:
```python
import jax
import jax.numpy as jnp
from jax import lax
from jax.sharding import PartitionSpec as P


def body(sigma_anc, panel_hat, pattern, diag_inverse):
    sigma_rows = lax.all_gather(sigma_anc, "col", axis=1, tiled=True)
    band_rows = sigma_rows.shape[0]
    ancestors = sigma_rows.shape[1]
    blocks = pattern.shape[0]
    block_width = ancestors // blocks
    row_start = lax.axis_index("row") * band_rows
    global_rows = row_start + lax.iota(jnp.int32, band_rows)
    row_onehot = (
        global_rows[:, None] // block_width == lax.iota(jnp.int32, blocks)[None, :]
    ).astype(jnp.float32)
    row_mask = jnp.dot(row_onehot, pattern.astype(jnp.float32), preferred_element_type=jnp.float32)
    expanded = jnp.broadcast_to(row_mask[:, :, None], (band_rows, blocks, block_width)).reshape(
        band_rows, ancestors
    )
    masked = sigma_rows * expanded
    product = jnp.dot(
        masked,
        lax.all_gather(panel_hat, "row", axis=0, tiled=True),
        precision=lax.Precision.HIGHEST,
        preferred_element_type=jnp.float32,
    )
    sigma_cross = -product
    partial_value = jnp.sum(panel_hat * sigma_cross, axis=0)
    summed = lax.psum(partial_value, "row")
    variance = diag_inverse - summed
    return (sigma_cross, variance)


def solution(mesh):
    in_specs = (P("row", "col"), P("row", "col"), P(), P("col"))
    out_specs = (P("row", "col"), P("col"))
    return jax.shard_map(body, mesh=mesh, in_specs=in_specs, out_specs=out_specs, check_vma=False)
```

profile of v0, /device:TPU:1, one launch (start us, length us, event | category | flops | bytes accessed | tf_op | source)
XLA Modules:
  0.0 368.6 jit_solution(3616185705939488497)
XLA Ops:
  7.2 0.0 copy-start.1
  7.2 0.0 all-gather.3.cloned.1.call-start
  7.2 0.7 all-gather.3.cloned.1.call-update
  7.9 0.0 all-gather.5.cloned.1.call-start
  8.0 0.7 all-gather.5.cloned.1.call-update
  8.7 1.0 fusion.3
  9.6 54.5 %all-gather.3.cloned.1.call-done = f32[128,8192]{1,0:T(8,128)} async-done(((f32[128,2048]{1,0:T(8,128)}), f32[128,8192]{1,0:T(8,128)}) %all-gather.3.cloned.1.call-update) | async-done | bytes 4194320 | tf_op jit(solution)/shard_map/all_gather | solution.py:8
  64.2 145.4 %all-gather.5.cloned.1.call-done = f32[8192,1024]{1,0:T(8,128)} async-done(((f32[128,1024]{1,0:T(8,128)}), f32[8192,1024]{1,0:T(8,128)}) %all-gather.5.cloned.1.call-update) | async-done | bytes 33554448 | tf_op jit(solution)/shard_map/all_gather | solution.py:25
  209.6 0.0 copy-start
  209.6 1.1 broadcast_in_dim.2
  210.7 0.0 copy-done.1
  210.7 1.0 copy-done
  211.7 0.0 copy-start.2
  211.8 25.7 %multiply_reduce_fusion = (f32[1024]{0:T(1024)S(1)}, f32[128,1024]{1,0:T(8,128)}) fusion(f32[128,1024]{1,0:T(8,128)S(1)} %copy-done.1, f32[8192,1024]{1,0:T(8,128)} %all-gather.5.cloned.1.call-done, f32[128,8192]{1,0:T(8,128)S(1)} %copy-done, f32[16,8,64,128]{3,2,1,0:T(8,128)S(1)} %bitcast.9), kind=kOutput, calls=%fused_computation.4 | convolution fusion | flops 12886342656 | bytes 42995712 | tf_op jit(solution)/shard_map/dot_general | solution.py:23
  237.5 123.7 %psum.7 = f32[1024]{0:T(1024)S(1)} all-reduce(f32[1024]{0:T(1024)S(1)} %get-tuple-element.2), channel_id=1, replica_groups=mesh['row'=64,'col'=4] {'row'}, use_global_device_ids=true, to_apply=%region_1.2 | all-reduce | flops 1024 | bytes 8192 | tf_op jit(solution)/shard_map/psum | solution.py:31
  361.1 0.0 copy-done.2
  361.1 0.6 sub.10
  (1 shorter events, 0.0 us)
Async XLA Ops:
  7.2 203.5 %copy-start.1 = (f32[128,1024]{1,0:T(8,128)S(1)}, f32[128,1024]{1,0:T(8,128)}, u32[]{:S(2)}) copy-start(f32[128,1024]{1,0:T(8,128)} %param.5) | copy-start | bytes 1572868
  7.2 57.0 %all-gather.3.cloned.1.call-start = ((), (), s32[]{:S(2)}) async-start(), calls=%async_computation | async-start | bytes 5242880 | tf_op jit(solution)/shard_map/all_gather | solution.py:8
  7.9 201.7 %all-gather.5.cloned.1.call-start = ((), (), s32[]{:S(2)}) async-start(), calls=%async_computation.1 | async-start | bytes 34078720 | tf_op jit(solution)/shard_map/all_gather | solution.py:25
  209.6 2.2 copy-start
  211.7 149.4 %copy-start.2 = (f32[1024]{0:T(1024)S(1)}, f32[1024]{0:T(1024)}, u32[]{:S(2)}) copy-start(f32[1024]{0:T(1024)} %param.7) | copy-start | bytes 12292
Sparse Core Ops, SparseCore 0:
  9.8 54.3 all-gather.2
  66.9 142.5 all-gather.4
where the time goes:
time: 369 us
  waiting for transfers between devices  201 us (54%)
  blocking collectives  124 us (34%)
  matrix products  26.7 us (7%)
  between operations  14.1 us (4%)
    all_gather x1, waiting for transfers between devices, body(): lax.all_gather(panel_hat, 'row', axis=0, tiled=True)  145 us
    psum x1, blocking collectives, body(): summed = lax.psum(partial_value, 'row')  124 us
    all_gather x1, waiting for transfers between devices, body(): sigma_rows = lax.all_gather(sigma_anc, 'col', axis=1, tiled=True)  54.5 us
    dot_general x1, matrix products, body(): jnp.dot(masked, lax.all_gather(panel_hat, 'row', axis=0, tiled=True), pre...  25.7 us
  transfers between devices with their start and end apart: 2, of which 2 were waited for; matrix products, arithmetic and copies ran while one was open for 0% of the time, Pallas kernels for 0%

commit v1 on v0

v1 whole, which is shorter than its diff:
```python
import functools
import heapq

import jax
import jax.numpy as jnp
from jax import lax
from jax.experimental import pallas as pl
from jax.experimental.pallas import tpu as pltpu
from jax.sharding import PartitionSpec as P

MESH = pl.DeviceIdType.MESH
NX, NY, NZ = 4, 4, 8
B = 128
W = 256
NS = 4
F32, BF16 = jnp.float32, jnp.bfloat16

LINK, LAT, CORE, CORE_LAT = 2.82, 1.8, 0.3, 1.0
T_ISSUE, T_PREP, T_TASK, T_SMALL = 0.06, 0.12, 1.2, 0.15


def hops(n, s):
    return 4 if (n % 2 == 0) == (s > 0) else 3


def plan():
    program, arrivals, free, done_at = [], [], {}, {}
    clock = [0.0]
    got, seq = set(), [0]

    def send(key, link, units=1.0):
        program.append(("send",) + key)
        clock[0] += T_ISSUE
        cost, lat = (CORE, CORE_LAT) if link == "c" else (LINK, LAT)
        start = max(clock[0], free.get(link, 0.0))
        free[link] = start + cost * units
        done_at[key] = free[link]
        seq[0] += 1
        heapq.heappush(arrivals, (free[link] + lat, seq[0], key))

    def sgn(s):
        return "+" if s > 0 else "-"

    def on(key):
        kind = key[0]
        if kind == "PZ":
            _, n, s, h = key
            if h < hops(n, s):
                send(("PZ", n, s, h + 1), "z" + sgn(s))
            send(("PC", n, (-s * h) % NZ), "c")
            if h == 2 and n + 2 < NS:
                send(("PZ", n + 2, s, 1), "z" + sgn(s))
                if s > 0:
                    send(("PC", n + 2, 0), "c")
        elif kind == "AR1":
            k = key[1]
            send(("AR2", k), "y" + "+-"[k])
        elif kind in ("AY", "AR2"):
            d, zz = ((-key[1]) % NY, key[2]) if kind == "AY" else (2, key[1])
            for s in (1, -1):
                send(("XS", d, zz, s, 1), "x" + sgn(s))
            got.add(("own", d, zz))
            if all(("own", e, f) in got for e in (1, 2, 3) for f in (0, 1)):
                for s in (1, -1):
                    send(("XS", 0, 1, s, 1), "x" + sgn(s))
        elif kind == "XS":
            _, d, zz, s, h = key
            if h == 1 and (zz == 0) == (s > 0):
                send(("XS", d, zz, s, 2), "x" + sgn(s))

    for s in (1, -1):
        send(("PZ", 0, s, 1), "z" + sgn(s))
        send(("AR1", 0 if s > 0 else 1), "y" + sgn(s))
        send(("XS", 0, 0, s, 1), "x" + sgn(s))
    send(("PC", 0, 0), "c")
    for s in (1, -1):
        send(("PZ", 1, s, 1), "z" + sgn(s))
        for zz in (0, 1):
            send(("AY", s, zz), "y" + sgn(s))
    send(("PC", 1, 0), "c")
    program.append(("local",))

    jobs = {}
    panel = {n: {("PZ", n, s, h) for s in (1, -1) for h in range(1, hops(n, s) + 1)} | {("PC", n, r) for r in range(NZ)} for n in range(NS)}
    rows = {}
    for d in range(NY):
        need = {("XS", d, zz, s, 1) for zz in (0, 1) for s in (1, -1)} | {("XS", d, 0, 1, 2), ("XS", d, 1, -1, 2)}
        need |= {0: set(), 2: {("AR2", 0), ("AR2", 1)}}.get(d, {("AY", 1 if d == 3 else -1, 0), ("AY", 1 if d == 3 else -1, 1)})
        rows[d] = need
    order = {2: 0, 1: 1, 3: 2, 0: 3}
    for d in range(NY):
        jobs[("prepA", d)] = (-1.0, rows[d], T_PREP * 8)
    for n in range(NS):
        jobs[("prepB", n)] = (-2.0, panel[n], T_PREP * 16)
        for d in range(NY):
            jobs[("task", d, n)] = (n + 0.1 * order[d], {("prepA", d), ("prepB", n)}, T_TASK)
        jobs[("y2", n)] = (-3.0, {("task", 2, n)}, 0.0)
        jobs[("y1", n, 1)] = (-3.0, {("task", 1, n), ("Y2", n, 1)}, T_SMALL)
        jobs[("y1", n, -1)] = (-3.0, {("task", 3, n), ("Y2", n, -1)}, T_SMALL)
        jobs[("fin", n)] = (-3.0, {("task", 0, n), ("Y1", n, 1), ("Y1", n, -1)}, T_SMALL)
    while jobs or arrivals:
        if arrivals and arrivals[0][0] <= clock[0]:
            key = heapq.heappop(arrivals)[2]
            program.append(("recv",) + key)
            clock[0] += T_ISSUE
            got.add(key)
            on(key)
            continue
        ready = [(p, j) for j, (p, need, _) in jobs.items() if need <= got]
        if ready:
            job = min(ready, key=lambda r: (r[0], str(r[1])))[1]
            program.append(job)
            clock[0] += jobs.pop(job)[2]
            got.add(job)
            if job[0] == "y2":
                for s in (1, -1):
                    send(("Y2", job[1], s), "y" + sgn(s), 0.5)
            elif job[0] == "y1":
                send(("Y1", job[1], job[2]), "y" + sgn(job[2]))
            continue
        late = sorted((t, k) for k, t in done_at.items() if t + 1.0 < clock[0])
        if late and arrivals and arrivals[0][0] > clock[0] + 0.05:
            program.append(("sent",) + late[0][1])
            del done_at[late[0][1]]
            clock[0] += 0.03
            continue
        clock[0] = max(clock[0], arrivals[0][0])
    for key in sorted(done_at, key=done_at.get):
        program.append(("sent",) + key)
    return program, clock[0]


def kernel(program, sem_of, pattern, sigma, panel, diag, cross, var, pbuf, sbuf, relay, a_hi, a_lo, b_hi, b_lo, part, r1, r2,
           va, vb, send_sem, recv_sem, va_send, va_recv, vb_send, vb_recv, local_sem):
    row, x = lax.axis_index("row"), lax.axis_index("col")
    z, y, c = row // (2 * NY), (row // 2) % NY, row % 2

    def at(dx=0, dy=0, dz=0, flip=False):
        core = 1 - c if flip else c
        return ((((z + dz + NZ) % NZ) * NY + (y + dy + NY) % NY) * 2 + core, (x + dx + NX) % NX)

    def lanes(start):
        return pl.ds(pl.multiple_of(start, W), W)

    def ends(key, sender):
        kind = key[0]
        if kind == "PZ":
            _, n, s, h = key
            zs = (z - s * (h - 1 if sender else h) + NZ) % NZ
            dst = pbuf.at[n, 2 * zs + c]
            src = panel.at[:, pl.ds(n * W, W)] if h == 1 else dst
            return src, dst, at(dz=s)
        if kind == "PC":
            _, n, rel = key
            zs = (z + rel) % NZ
            dst = pbuf.at[n, 2 * zs + (c if sender else 1 - c)]
            src = panel.at[:, pl.ds(n * W, W)] if rel == 0 else dst
            return src, dst, at(flip=True)
        if kind == "AY":
            _, s, zz = key
            src = sigma.at[:, lanes(zz * NY * W + ((y + s + NY) % NY) * W)]
            return src, sbuf.at[(-s) % NY, 2 * x + zz], at(dy=s)
        if kind == "AR1":
            k = key[1]
            src = sigma.at[:, lanes(k * NY * W + ((y + 2) % NY) * W)]
            return src, relay.at[k], at(dy=1 - 2 * k)
        if kind == "AR2":
            k = key[1]
            return relay.at[k], sbuf.at[2, 2 * x + k], at(dy=1 - 2 * k)
        if kind == "XS":
            _, d, zz, s, h = key
            xs = (x - s * (h - 1 if sender else h) + NX) % NX
            dst = sbuf.at[d, 2 * xs + zz]
            src = sigma.at[:, lanes(zz * NY * W + y * W)] if d == 0 and h == 1 else dst
            return src, dst, at(dx=s)
        if kind == "Y2":
            _, n, s = key
            i = 0 if s > 0 else 1
            return part.at[2, n, pl.ds(i * (B // 2), B // 2)], r1.at[i, n], at(dy=s)
        _, n, s = key
        return part.at[s % NY, n], r2.at[0 if s > 0 else 1, n], at(dy=s)

    def copy(key, sender):
        src, dst, target = ends(key, sender)
        i = sem_of[key]
        return pltpu.make_async_remote_copy(
            src_ref=src if sender else dst, dst_ref=dst, send_sem=send_sem.at[i], recv_sem=recv_sem.at[i], device_id=target,
            device_id_type=MESH)

    barrier = pltpu.get_barrier_semaphore()
    me8 = row % (2 * NY)
    group = [(z * 2 * NY + (me8 + r) % (2 * NY), x) for r in range(1, 2 * NY)]
    stack = [at(dz=r) for r in range(1, NZ)]
    peers = group + stack + [at(dx=1), at(dx=-1)]
    for peer in peers:
        pl.semaphore_signal(barrier, inc=1, device_id=peer, device_id_type=MESH)
    pl.semaphore_wait(barrier, len(peers))

    locals_ = [pltpu.make_async_copy(panel.at[:, pl.ds(n * W, W)], pbuf.at[n, 2 * z + c], local_sem.at[n]) for n in range(NS)]
    locals_ += [pltpu.make_async_copy(sigma.at[:, lanes(zz * NY * W + y * W)], sbuf.at[0, 2 * x + zz], local_sem.at[NS + zz]) for zz in (0, 1)]

    def prep_a(d):
        if d == 0:
            for zz in (0, 1):
                locals_[NS + zz].wait()
        rb = (z * NY + (y + d) % NY) * 2 + c

        def one(zk, carry):
            cb = (zk * NY + y) * 2
            for j in (0, 1):
                m = pattern[rb, cb + j].astype(F32)
                s = sbuf[d, zk, :, pl.ds(j * B, B)] * m
                hi = s.astype(BF16)
                a_hi[zk, pl.ds(d * B, B), pl.ds(j * B, B)] = hi
                a_lo[zk, pl.ds(d * B, B), pl.ds(j * B, B)] = (s - hi.astype(F32)).astype(BF16)
            return carry

        lax.fori_loop(0, NZ, one, 0)

    def prep_b(n):
        locals_[n].wait()

        def one(k, carry):
            for j in (0, 1):
                p = pbuf[n, 2 * k + j]
                hi = p.astype(BF16)
                b_hi[n, k, pl.ds(j * B, B)] = hi
                b_lo[n, k, pl.ds(j * B, B)] = (p - hi.astype(F32)).astype(BF16)
            return carry

        lax.fori_loop(0, NZ, one, 0)

    def task(d, n):
        def one(k, acc):
            hi, lo = a_hi[k, pl.ds(d * B, B)], a_lo[k, pl.ds(d * B, B)]
            dot = functools.partial(jnp.dot, preferred_element_type=F32)
            return acc + (dot(hi, b_hi[n, k]) + (dot(hi, b_lo[n, k]) + dot(lo, b_hi[n, k])))

        part[d, n] = lax.fori_loop(0, NZ, one, jnp.zeros((B, W), F32))

    for act in program:
        kind = act[0]
        if kind == "send":
            copy(act[1:], True).start()
        elif kind == "recv":
            copy(act[1:], False).wait_recv()
        elif kind == "sent":
            copy(act[1:], True).wait_send()
        elif kind == "local":
            for cp in locals_:
                cp.start()
        elif kind == "prepA":
            prep_a(act[1])
        elif kind == "prepB":
            prep_b(act[1])
        elif kind == "task":
            task(act[1], act[2])
        elif kind == "y1":
            _, n, s = act
            i = 0 if s > 0 else 1
            half = pl.ds(i * (B // 2), B // 2)
            part[s % NY, n, half] = part[s % NY, n, half] + r1[i, n]
        elif kind == "fin":
            n = act[1]
            out = -(part[0, n] + (r2[0, n] + r2[1, n]))
            cross[:, pl.ds(n * W, W)] = out
            prod = jnp.sum(out * pbuf[n, 2 * z + c], axis=0, keepdims=True)
            for j in (0, 1):
                va[me8, pl.ds(2 * n + j, 1)] = prod[:, j * B:(j + 1) * B]

    def exchange(buf, mine, members, n, ssem, rsem, base):
        cps = []
        for r in range(1, n):
            cps.append(pltpu.make_async_remote_copy(
                src_ref=buf.at[mine], dst_ref=buf.at[mine], send_sem=ssem.at[r], recv_sem=rsem.at[r], device_id=members[r - 1],
                device_id_type=MESH))
            cps[-1].start()
        for r in range(1, n):
            slot = buf.at[(mine - r + n) % n]
            pltpu.make_async_remote_copy(
                src_ref=slot, dst_ref=slot, send_sem=ssem.at[r], recv_sem=rsem.at[r], device_id=members[r - 1],
                device_id_type=MESH).wait_recv()
        total = buf[0]
        for i in range(1, n):
            total = total + buf[i]
        return total, cps

    total, first = exchange(va, me8, group, 2 * NY, va_send, va_recv, 0)
    vb[z] = total
    total, second = exchange(vb, z, stack, NZ, vb_send, vb_recv, 0)
    var[...] = diag[...] - total
    for cp in first + second:
        cp.wait_send()


def body(sigma_anc, panel_hat, pattern, diag_inverse):
    program, _ = plan()
    keys = sorted({act[1:] for act in program if act[0] == "send"}, key=str)
    sem_of = {key: i for i, key in enumerate(keys)}
    dma = pltpu.SemaphoreType.DMA
    vmem = pl.BlockSpec(memory_space=pltpu.VMEM)
    anywhere = pl.BlockSpec(memory_space=pl.ANY)
    cross, var = pl.pallas_call(
        functools.partial(kernel, program, sem_of),
        out_shape=(jax.ShapeDtypeStruct((B, NS * W), F32), jax.ShapeDtypeStruct((8, B), F32)),
        in_specs=[pl.BlockSpec(memory_space=pltpu.SMEM), anywhere, anywhere, vmem],
        out_specs=(vmem, vmem),
        scratch_shapes=[
            pltpu.VMEM((NS, 2 * NZ, B, W), F32),
            pltpu.VMEM((NY, NZ, B, W), F32),
            pltpu.VMEM((2, B, W), F32),
            pltpu.VMEM((NZ, NY * B, W), BF16),
            pltpu.VMEM((NZ, NY * B, W), BF16),
            pltpu.VMEM((NS, NZ, W, W), BF16),
            pltpu.VMEM((NS, NZ, W, W), BF16),
            pltpu.VMEM((NY, NS, B, W), F32),
            pltpu.VMEM((2, NS, B // 2, W), F32),
            pltpu.VMEM((2, NS, B, W), F32),
            pltpu.VMEM((2 * NY, 8, B), F32),
            pltpu.VMEM((NZ, 8, B), F32),
            dma((len(keys),)),
            dma((len(keys),)),
            dma((2 * NY,)),
            dma((2 * NY,)),
            dma((NZ,)),
            dma((NZ,)),
            dma((NS + 2,)),
        ],
        compiler_params=pltpu.CompilerParams(collective_id=0, has_side_effects=True, vmem_limit_bytes=56 * 1024 * 1024),
        name="selected_inverse",
    )(pattern, sigma_anc, panel_hat, diag_inverse.reshape(8, B))
    return cross, var.reshape(-1)


def solution(mesh):
    in_specs = (P("row", "col"), P("row", "col"), P(), P("col"))
    out_specs = (P("row", "col"), P("col"))
    return jax.shard_map(body, mesh=mesh, in_specs=in_specs, out_specs=out_specs, check_vma=False)
```

time: 369 us -> 101 us (0.27)
  waiting for transfers between devices: 201 us -> 0 us
  blocking collectives: 124 us -> 0 us
  Pallas kernels: 0 us -> 98.1 us
  matrix products: 26.7 us -> 0 us
  between operations: 14.1 us -> 0.65 us
    all_gather x2 -> x0, waiting for transfers between devices: 200 us -> none  [the longest x1 145 us: body(): lax.all_gather(panel_hat, 'row', axis=0, tiled=True)]
    psum x1 -> x0, blocking collectives: 124 us -> none  [body(): summed = lax.psum(partial_value, 'row')]
    pallas_call x0 -> x1, Pallas kernels: none -> 98.1 us  [body(): pl.pallas_call(functools.partial(kernel, program, sem_of), out_shape=(jax...]
    dot_general x2 -> x0, matrix products: 26.7 us -> none  [the longest x1 25.7 us: body(): jnp.dot(masked, lax.all_gather(panel_hat, 'row', axis=0, tiled=True), pre...]
  transfers between devices with their start and end apart: 2 -> 0, of which waited for: 2 -> 0; matrix products, arithmetic and copies ran while one was open for 0% -> 0% of each run, Pallas kernels for 0% -> 0%
where the time goes in v1:
time: 101 us
  Pallas kernels  98.1 us (97%)
  local copies, waits for them, and re-layouts  2.48 us (2%)
    pallas_call x1, Pallas kernels, body(): pl.pallas_call(functools.partial(kernel, program, sem_of), out_shape=(jax...  98.1 us
    unnamed x4, local copies, waits for them, and re-layouts  2.48 us

profile of v1, /device:TPU:1, one launch (start us, length us, event | category | flops | bytes accessed | tf_op | source)
XLA Modules:
  0.0 101.2 jit_solution(13499598108032230347)
XLA Ops:
  0.6 98.1 %selected_inverse.1 = (f32[128,1024]{1,0:T(8,128)}, f32[8,128]{1,0:T(8,128)}) custom-call(s32[64,64]{1,0:T(8,128)} %pattern.1, f32[128,2048]{1,0:T(8,128)} %sigma.1, f32[128,1024]{1,0:T(8,128)} %panel.1, f32[8,128]{1,0:T(8,128)} %bitcast.2), custom_call_target="tpu_custom_call" | custom-call | tf_op jit(solution)/shard_map/selected_inverse/pallas_call | solution.py:303
  98.7 0.0 copy-start
  98.7 1.9 %copy.8 = f32[128,1024]{1,0:T(8,128)} copy(f32[128,1024]{1,0:T(8,128)} %get-tuple-element.8) | data formatting | bytes 1048576
  100.6 0.0 copy-done
  100.6 0.6 copy.9
Async XLA Ops:
  98.7 1.9 %copy-start = (f32[8,128]{1,0:T(8,128)S(1)}, f32[8,128]{1,0:T(8,128)}, u32[]{:S(2)}) copy-start(f32[8,128]{1,0:T(8,128)} %get-tuple-element.5) | copy-start | bytes 12292

commit v2 on v1

--- a/solution.py
+++ b/solution.py
@@ -16,7 +16,9 @@
 F32, BF16 = jnp.float32, jnp.bfloat16
 
 LINK, LAT, CORE, CORE_LAT = 2.82, 1.8, 0.3, 1.0
-T_ISSUE, T_PREP, T_TASK, T_SMALL = 0.06, 0.12, 1.2, 0.15
+T_ISSUE, T_PREP, T_TASK, T_SMALL, T_STEP = 0.03, 0.035, 0.96, 0.1, 0.45
+LAST = NS - 1
+VA_LAT, VB_LAT = 2.6, 4.2
 
 
 def hops(n, s):
@@ -31,7 +33,7 @@
     def send(key, link, units=1.0):
         program.append(("send",) + key)
         clock[0] += T_ISSUE
-        cost, lat = (CORE, CORE_LAT) if link == "c" else (LINK, LAT)
+        cost, lat = {"c": (CORE, CORE_LAT), "va": (0.0, VA_LAT), "vb": (0.0, VB_LAT)}.get(link, (LINK, LAT))
         start = max(clock[0], free.get(link, 0.0))
         free[link] = start + cost * units
         done_at[key] = free[link]
@@ -55,14 +57,14 @@
         elif kind == "AR1":
             k = key[1]
             send(("AR2", k), "y" + "+-"[k])
+            send(("AY", 1 - 2 * k, 1), "y" + "+-"[k])
+            send(("PY", 1 - 2 * k, 1), "y" + "+-"[k])
+        elif kind == "PY" and key[2] == 1:
+            send(("PY", key[1], 2), "y" + sgn(key[1]), 0.5)
         elif kind in ("AY", "AR2"):
             d, zz = ((-key[1]) % NY, key[2]) if kind == "AY" else (2, key[1])
             for s in (1, -1):
                 send(("XS", d, zz, s, 1), "x" + sgn(s))
-            got.add(("own", d, zz))
-            if all(("own", e, f) in got for e in (1, 2, 3) for f in (0, 1)):
-                for s in (1, -1):
-                    send(("XS", 0, 1, s, 1), "x" + sgn(s))
         elif kind == "XS":
             _, d, zz, s, h = key
             if h == 1 and (zz == 0) == (s > 0):
@@ -74,9 +76,9 @@
         send(("XS", 0, 0, s, 1), "x" + sgn(s))
     send(("PC", 0, 0), "c")
     for s in (1, -1):
+        send(("XS", 0, 1, s, 1), "x" + sgn(s))
         send(("PZ", 1, s, 1), "z" + sgn(s))
-        for zz in (0, 1):
-            send(("AY", s, zz), "y" + sgn(s))
+        send(("AY", s, 0), "y" + sgn(s))
     send(("PC", 1, 0), "c")
     program.append(("local",))
 
@@ -90,10 +92,22 @@
     order = {2: 0, 1: 1, 3: 2, 0: 3}
     for d in range(NY):
         jobs[("prepA", d)] = (-1.0, rows[d], T_PREP * 8)
+    for rel in range(NZ):
+        units = {("PC", LAST, rel)}
+        if rel:
+            units |= {("PZ", LAST, s, h) for s in (1, -1) for h in range(1, hops(LAST, s) + 1) if (-s * h) % NZ == rel}
+        jobs[("step", rel)] = (LAST - 0.5, {("prepA", d) for d in range(NY)} | units | ({("step", 0)} if rel else set()), T_STEP)
+    jobs[("vlast",)] = (-4.0, {("step", rel) for rel in range(NZ)} | {("PY", s, h) for s in (1, -1) for h in (1, 2)} | {("fin", n) for n in range(LAST)}, 0.5)
+    jobs[("vsum",)] = (-4.0, {("VA", r) for r in range(1, 2 * NY)}, 0.05)
+    jobs[("vend",)] = (-4.0, {("VB", r) for r in range(1, NZ)}, 0.05)
     for n in range(NS):
-        jobs[("prepB", n)] = (-2.0, panel[n], T_PREP * 16)
-        for d in range(NY):
-            jobs[("task", d, n)] = (n + 0.1 * order[d], {("prepA", d), ("prepB", n)}, T_TASK)
+        if n < LAST:
+            jobs[("prepB", n)] = (-2.0, panel[n], T_PREP * 16)
+            for d in range(NY):
+                jobs[("task", d, n)] = (n + 0.1 * order[d], {("prepA", d), ("prepB", n)}, T_TASK)
+        else:
+            for d in range(NY):
+                jobs[("task", d, n)] = (-3.5, {("vlast",)}, 0.0)
         jobs[("y2", n)] = (-3.0, {("task", 2, n)}, 0.0)
         jobs[("y1", n, 1)] = (-3.0, {("task", 1, n), ("Y2", n, 1)}, T_SMALL)
         jobs[("y1", n, -1)] = (-3.0, {("task", 3, n), ("Y2", n, -1)}, T_SMALL)
@@ -115,10 +129,16 @@
             if job[0] == "y2":
                 for s in (1, -1):
                     send(("Y2", job[1], s), "y" + sgn(s), 0.5)
+            elif job[0] == "vlast":
+                for r in range(1, 2 * NY):
+                    send(("VA", r), "va")
+            elif job[0] == "vsum":
+                for r in range(1, NZ):
+                    send(("VB", r), "vb")
             elif job[0] == "y1":
                 send(("Y1", job[1], job[2]), "y" + sgn(job[2]))
             continue
-        late = sorted((t, k) for k, t in done_at.items() if t + 1.0 < clock[0])
+        late = sorted((t, k) for k, t in done_at.items() if t + 3.0 < clock[0])
         if late and arrivals and arrivals[0][0] > clock[0] + 0.05:
             program.append(("sent",) + late[0][1])
             del done_at[late[0][1]]
@@ -127,11 +147,11 @@
         clock[0] = max(clock[0], arrivals[0][0])
     for key in sorted(done_at, key=done_at.get):
         program.append(("sent",) + key)
-    return program, clock[0]
-
-
-def kernel(program, sem_of, pattern, sigma, panel, diag, cross, var, pbuf, sbuf, relay, a_hi, a_lo, b_hi, b_lo, part, r1, r2,
-           va, vb, send_sem, recv_sem, va_send, va_recv, vb_send, vb_recv, local_sem):
+    return program, clock[0], free
+
+
+def kernel(program, sem_of, pattern_hbm, sigma, panel, cross, var, pattern, pbuf, sbuf, relay, a_hi, a_lo, b_hi, b_lo, part, r1, r2,
+           pv, obuf, va, vb, send_sem, recv_sem, local_sem, out_sem):
     row, x = lax.axis_index("row"), lax.axis_index("col")
     z, y, c = row // (2 * NY), (row // 2) % NY, row % 2
 
@@ -173,12 +193,24 @@
             dst = sbuf.at[d, 2 * xs + zz]
             src = sigma.at[:, lanes(zz * NY * W + y * W)] if d == 0 and h == 1 else dst
             return src, dst, at(dx=s)
+        if kind == "PY":
+            _, s, h = key
+            if h == 1:
+                return panel.at[:, pl.ds(LAST * W, W)], pv.at[(-s) % NY], at(dy=s)
+            half = pl.ds((0 if s > 0 else 1) * (B // 2), B // 2)
+            return pv.at[(-s) % NY, half], pv.at[2, half], at(dy=s)
+        if kind == "VA":
+            slot = va.at[me8 if sender else (me8 - key[1] + 2 * NY) % (2 * NY)]
+            return slot, slot, (z * 2 * NY + (me8 + key[1]) % (2 * NY), x)
+        if kind == "VB":
+            slot = vb.at[z if sender else (z - key[1] + NZ) % NZ]
+            return slot, slot, at(dz=key[1])
         if kind == "Y2":
             _, n, s = key
             i = 0 if s > 0 else 1
-            return part.at[2, n, pl.ds(i * (B // 2), B // 2)], r1.at[i, n], at(dy=s)
+            return part.at[n, 2, pl.ds(i * (B // 2), B // 2)], r1.at[i, n], at(dy=s)
         _, n, s = key
-        return part.at[s % NY, n], r2.at[0 if s > 0 else 1, n], at(dy=s)
+        return part.at[n, s % NY], r2.at[0 if s > 0 else 1, n], at(dy=s)
 
     def copy(key, sender):
         src, dst, target = ends(key, sender)
@@ -187,22 +219,17 @@
             src_ref=src if sender else dst, dst_ref=dst, send_sem=send_sem.at[i], recv_sem=recv_sem.at[i], device_id=target,
             device_id_type=MESH)
 
+    me8 = row % (2 * NY)
     barrier = pltpu.get_barrier_semaphore()
-    me8 = row % (2 * NY)
-    group = [(z * 2 * NY + (me8 + r) % (2 * NY), x) for r in range(1, 2 * NY)]
-    stack = [at(dz=r) for r in range(1, NZ)]
-    peers = group + stack + [at(dx=1), at(dx=-1)]
+    peers = [at(dx=1), at(dx=-1), at(dy=1), at(dy=-1), at(dz=1), at(dz=-1), at(flip=True)]
     for peer in peers:
         pl.semaphore_signal(barrier, inc=1, device_id=peer, device_id_type=MESH)
-    pl.semaphore_wait(barrier, len(peers))
-
     locals_ = [pltpu.make_async_copy(panel.at[:, pl.ds(n * W, W)], pbuf.at[n, 2 * z + c], local_sem.at[n]) for n in range(NS)]
     locals_ += [pltpu.make_async_copy(sigma.at[:, lanes(zz * NY * W + y * W)], sbuf.at[0, 2 * x + zz], local_sem.at[NS + zz]) for zz in (0, 1)]
+    locals_ += [pltpu.make_async_copy(pattern_hbm, pattern, local_sem.at[NS + 2])]
+    pl.semaphore_wait(barrier, len(peers))
 
     def prep_a(d):
-        if d == 0:
-            for zz in (0, 1):
-                locals_[NS + zz].wait()
         rb = (z * NY + (y + d) % NY) * 2 + c
 
         def one(zk, carry):
@@ -217,26 +244,41 @@
 
         lax.fori_loop(0, NZ, one, 0)
 
+    def split_b(n, k):
+        for j in (0, 1):
+            p = pbuf[n, 2 * k + j]
+            hi = p.astype(BF16)
+            b_hi[n, k, pl.ds(j * B, B)] = hi
+            b_lo[n, k, pl.ds(j * B, B)] = (p - hi.astype(F32)).astype(BF16)
+
     def prep_b(n):
-        locals_[n].wait()
-
         def one(k, carry):
-            for j in (0, 1):
-                p = pbuf[n, 2 * k + j]
-                hi = p.astype(BF16)
-                b_hi[n, k, pl.ds(j * B, B)] = hi
-                b_lo[n, k, pl.ds(j * B, B)] = (p - hi.astype(F32)).astype(BF16)
+            split_b(n, k)
             return carry
 
         lax.fori_loop(0, NZ, one, 0)
 
+    dot = functools.partial(jnp.dot, preferred_element_type=F32)
+
     def task(d, n):
-        def one(k, acc):
+        acc = jnp.zeros((B, W), F32)
+        for k in range(NZ):
             hi, lo = a_hi[k, pl.ds(d * B, B)], a_lo[k, pl.ds(d * B, B)]
-            dot = functools.partial(jnp.dot, preferred_element_type=F32)
-            return acc + (dot(hi, b_hi[n, k]) + (dot(hi, b_lo[n, k]) + dot(lo, b_hi[n, k])))
-
-        part[d, n] = lax.fori_loop(0, NZ, one, jnp.zeros((B, W), F32))
+            acc = acc + (dot(hi, b_hi[n, k]) + (dot(hi, b_lo[n, k]) + dot(lo, b_hi[n, k])))
+        part[n, d] = acc
+
+    def step(rel):
+        k = (z + rel) % NZ
+        split_b(LAST, k)
+        hi, lo = a_hi[k], a_lo[k]
+        res = (dot(hi, b_hi[LAST, k]) + (dot(hi, b_lo[LAST, k]) + dot(lo, b_hi[LAST, k]))).reshape(NY, B, W)
+        part[LAST] = part[LAST] + res if rel else res
+
+    def put_var(n, prod):
+        for j in (0, 1):
+            va[me8, pl.ds(2 * n + j, 1)] = prod[:, j * B:(j + 1) * B]
+
+    outs = [pltpu.make_async_copy(obuf.at[n], cross.at[:, pl.ds(n * W, W)], out_sem.at[n]) for n in range(NS)]
 
     for act in program:
         kind = act[0]
@@ -249,52 +291,50 @@
         elif kind == "local":
             for cp in locals_:
                 cp.start()
+            for cp in locals_:
+                cp.wait()
         elif kind == "prepA":
             prep_a(act[1])
         elif kind == "prepB":
             prep_b(act[1])
         elif kind == "task":
-            task(act[1], act[2])
+            if act[2] < LAST:
+                task(act[1], act[2])
+        elif kind == "step":
+            step(act[1])
         elif kind == "y1":
             _, n, s = act
             i = 0 if s > 0 else 1
             half = pl.ds(i * (B // 2), B // 2)
-            part[s % NY, n, half] = part[s % NY, n, half] + r1[i, n]
+            part[n, s % NY, half] = part[n, s % NY, half] + r1[i, n]
         elif kind == "fin":
             n = act[1]
-            out = -(part[0, n] + (r2[0, n] + r2[1, n]))
-            cross[:, pl.ds(n * W, W)] = out
-            prod = jnp.sum(out * pbuf[n, 2 * z + c], axis=0, keepdims=True)
-            for j in (0, 1):
-                va[me8, pl.ds(2 * n + j, 1)] = prod[:, j * B:(j + 1) * B]
-
-    def exchange(buf, mine, members, n, ssem, rsem, base):
-        cps = []
-        for r in range(1, n):
-            cps.append(pltpu.make_async_remote_copy(
-                src_ref=buf.at[mine], dst_ref=buf.at[mine], send_sem=ssem.at[r], recv_sem=rsem.at[r], device_id=members[r - 1],
-                device_id_type=MESH))
-            cps[-1].start()
-        for r in range(1, n):
-            slot = buf.at[(mine - r + n) % n]
-            pltpu.make_async_remote_copy(
-                src_ref=slot, dst_ref=slot, send_sem=ssem.at[r], recv_sem=rsem.at[r], device_id=members[r - 1],
-                device_id_type=MESH).wait_recv()
-        total = buf[0]
-        for i in range(1, n):
-            total = total + buf[i]
-        return total, cps
-
-    total, first = exchange(va, me8, group, 2 * NY, va_send, va_recv, 0)
-    vb[z] = total
-    total, second = exchange(vb, z, stack, NZ, vb_send, vb_recv, 0)
-    var[...] = diag[...] - total
-    for cp in first + second:
-        cp.wait_send()
+            out = part[n, 0] + (r2[0, n] + r2[1, n])
+            obuf[n] = out
+            outs[n].start()
+            if n < LAST:
+                put_var(n, jnp.sum(out * pbuf[n, 2 * z + c], axis=0, keepdims=True))
+        elif kind == "vlast":
+            prod = part[LAST, 0] * pbuf[LAST, 2 * z + c]
+            for d in range(1, NY):
+                prod = prod + part[LAST, d] * pv[d]
+            put_var(LAST, jnp.sum(prod, axis=0, keepdims=True))
+        elif kind == "vsum":
+            total = va[0]
+            for i in range(1, 2 * NY):
+                total = total + va[i]
+            vb[z] = total
+        elif kind == "vend":
+            total = vb[0]
+            for i in range(1, NZ):
+                total = total + vb[i]
+            var[...] = total
+    for cp in outs:
+        cp.wait()
 
 
 def body(sigma_anc, panel_hat, pattern, diag_inverse):
-    program, _ = plan()
+    program = plan()[0]
     keys = sorted({act[1:] for act in program if act[0] == "send"}, key=str)
     sem_of = {key: i for i, key in enumerate(keys)}
     dma = pltpu.SemaphoreType.DMA
@@ -302,10 +342,11 @@
     anywhere = pl.BlockSpec(memory_space=pl.ANY)
     cross, var = pl.pallas_call(
         functools.partial(kernel, program, sem_of),
-        out_shape=(jax.ShapeDtypeStruct((B, NS * W), F32), jax.ShapeDtypeStruct((8, B), F32)),
-        in_specs=[pl.BlockSpec(memory_space=pltpu.SMEM), anywhere, anywhere, vmem],
+        out_shape=(pltpu.VMEM((B, NS * W), F32), pltpu.VMEM((8, B), F32)),
+        in_specs=[pl.BlockSpec(memory_space=pltpu.HBM)] * 3,
         out_specs=(vmem, vmem),
         scratch_shapes=[
+            pltpu.SMEM((NY * NZ * 2, NY * NZ * 2), jnp.int32),
             pltpu.VMEM((NS, 2 * NZ, B, W), F32),
             pltpu.VMEM((NY, NZ, B, W), F32),
             pltpu.VMEM((2, B, W), F32),
@@ -313,23 +354,22 @@
             pltpu.VMEM((NZ, NY * B, W), BF16),
             pltpu.VMEM((NS, NZ, W, W), BF16),
             pltpu.VMEM((NS, NZ, W, W), BF16),
-            pltpu.VMEM((NY, NS, B, W), F32),
+            pltpu.VMEM((NS, NY, B, W), F32),
             pltpu.VMEM((2, NS, B // 2, W), F32),
             pltpu.VMEM((2, NS, B, W), F32),
+            pltpu.VMEM((NY, B, W), F32),
+            pltpu.VMEM((NS, B, W), F32),
             pltpu.VMEM((2 * NY, 8, B), F32),
             pltpu.VMEM((NZ, 8, B), F32),
             dma((len(keys),)),
             dma((len(keys),)),
-            dma((2 * NY,)),
-            dma((2 * NY,)),
-            dma((NZ,)),
-            dma((NZ,)),
-            dma((NS + 2,)),
+            dma((NS + 3,)),
+            dma((NS,)),
         ],
         compiler_params=pltpu.CompilerParams(collective_id=0, has_side_effects=True, vmem_limit_bytes=56 * 1024 * 1024),
         name="selected_inverse",
-    )(pattern, sigma_anc, panel_hat, diag_inverse.reshape(8, B))
-    return cross, var.reshape(-1)
+    )(pattern, sigma_anc, panel_hat)
+    return -cross, diag_inverse + var.reshape(-1)
 
 
 def solution(mesh):

time: 101 us -> 79.2 us (0.78)
  Pallas kernels: 98.1 us -> 76.9 us
  local copies, waits for them, and re-layouts: 2.48 us -> 0.01 us
  other arithmetic: 0 us -> 1.43 us
    pallas_call x1, Pallas kernels: 98.1 us -> 76.9 us  [body(): pl.pallas_call(functools.partial(kernel, program, sem_of), out_shape=(plt...]
    unnamed x4 -> x2, local copies, waits for them, and re-layouts: 2.48 us -> 0.01 us
where the time goes in v2:
time: 79.2 us; the launch traced here: 78.9 us
  Pallas kernels  76.9 us (97%)
  other arithmetic  1.43 us (2%)
    pallas_call x1, Pallas kernels, body(): pl.pallas_call(functools.partial(kernel, program, sem_of), out_shape=(plt...  76.9 us

profile of v2, /device:TPU:1, one launch (start us, length us, event | category | flops | bytes accessed | tf_op | source)
XLA Modules:
  0.0 78.9 jit_solution(7296052765934364186)
XLA Ops:
  0.6 76.9 %selected_inverse.1 = (f32[128,1024]{1,0:T(8,128)S(1)}, f32[8,128]{1,0:T(8,128)S(1)}) custom-call(s32[64,64]{1,0:T(8,128)} %pattern_hbm.1, f32[128,2048]{1,0:T(8,128)} %sigma.1, f32[128,1024]{1,0:T(8,128)} %panel.1), custom_call_target="tpu_custom_call" | custom-call | tf_op jit(solution)/shard_map/selected_inverse/pallas_call | solution.py:343
  77.5 0.0 copy-start
  77.5 0.8 %neg.3 = f32[128,1024]{1,0:T(8,128)} negate(f32[128,1024]{1,0:T(8,128)S(1)} %get-tuple-element.4) | non-fusion elementwise | flops 131072 | bytes 1048576 | tf_op jit(solution)/shard_map/neg | solution.py:372
  78.3 0.0 copy-done
  78.3 0.6 bitcast_add_fusion
Async XLA Ops:
  77.5 0.9 %copy-start = (f32[1024]{0:T(1024)S(1)}, f32[1024]{0:T(1024)}, u32[]{:S(2)}) copy-start(f32[1024]{0:T(1024)} %param.7) | copy-start | bytes 12292

commit v3 on v2

v3 whole, which is shorter than its diff:
```python
import functools
import heapq

import jax
import jax.numpy as jnp
from jax import lax
from jax.experimental import pallas as pl
from jax.experimental.pallas import tpu as pltpu
from jax.sharding import PartitionSpec as P

MESH = pl.DeviceIdType.MESH
NX, NY, NZ = 4, 4, 8
B = 128
W = 256
NS = 4
F32, BF16 = jnp.float32, jnp.bfloat16

EARLY = (2, 3)
STEPPED = (2, 3)
LATE_D = 1
POS = (0, 3, 1, 2)
FAR = NZ // 2
SEND_POOL = 40
Y_SHARED = 25.0
X_WINDOW = 2
NEXT = (None, (1, 2), (2, 3), (1, 2))

LINK, LAT, CORE, CORE_LAT = 2.82, 2.0, 0.3, 1.0
T_ISSUE, T_PREP, T_TASK, T_SMALL, T_STEP, T_BLOCK = 0.03, 0.035, 0.96, 0.1, 0.5, 0.4
VZ_LAT, VG_LAT = 4.2, 3.0
D_ORDER = (0, 2, 3, 1)


def subs(s, h):
    first = 0 if s > 0 else 1
    return (first,) if h == FAR else (first, 1 - first)


def sgn(s):
    return "+" if s > 0 else "-"


def plan():
    program, arrivals, free, done_at = [], [], {}, {}
    clock = [0.0]
    got, seq, ends = set(), [0], {}

    def send(key, link, units=1.0):
        program.append(("send",) + key)
        clock[0] += T_ISSUE
        cost, lat = {"c": (CORE, CORE_LAT), "vz": (0.0, VZ_LAT), "vg": (0.0, VG_LAT)}.get(link, (LINK, LAT))
        start = max(clock[0], free.get(link, 0.0))
        took = cost * units
        if link[0] == "y" and clock[0] > Y_SHARED:
            both = min(max(free.get("y+" if link == "y-" else "y-", 0.0) - start, 0.0), took)
            took = (took + both) / 2
        free[link] = start + took
        done_at[key] = ends[key] = free[link]
        seq[0] += 1
        heapq.heappush(arrivals, (free[link] + lat, seq[0], key))

    def pz(n, s, h, sub):
        send(("PZ", n, s, h, sub), "z" + sgn(s), 0.5)

    def start_slice(n, s):
        for sub in subs(s, 1):
            pz(n, s, 1, sub)

    order = {d: i for i, d in enumerate(D_ORDER)}
    held, under_way = [], {(0, 0): 2, (0, 1): 2}

    def forward_x():
        while held and len(under_way) < X_WINDOW:
            d, zz = min(held, key=lambda e: (order[e[0]], e[1]))
            if any(("own", e, f) not in got for e in D_ORDER[1:order[d]] for f in (0, 1)):
                return
            held.remove((d, zz))
            got.add(("own", d, zz))
            under_way[(d, zz)] = 2
            for s in (1, -1):
                send(("XS", d, zz, s, 1), "x" + sgn(s))

    def on(key):
        kind = key[0]
        if kind == "PZ":
            _, n, s, h, sub = key
            if h < FAR and sub in subs(s, h + 1):
                pz(n, s, h + 1, sub)
            if h == FAR:
                send(("PC", n, FAR, sub + 1), "c", 0.5)
            elif sub == subs(s, h)[1]:
                send(("PC", n, (-s * h) % NZ, 0), "c")
            for i, after in enumerate(NEXT[n + 1] if n + 1 < NS else ()):
                if (h, sub) == (after, subs(s, h)[0]):
                    pz(n + 1, s, 1, subs(s, 1)[i])
                    if s > 0 and i:
                        send(("PC", n + 1, 0, 0), "c")
        elif kind == "AR1":
            k = key[1]
            y = "y" + "+-"[k]
            send(("AR2", k), y)
            for zz in (0, 1):
                send(("AY", 1 - 2 * k, zz), y)
            for n in EARLY:
                send(("PY", n, 1 - 2 * k, 1), y)
        elif kind == "PY" and key[3] == 1:
            send(("PY", key[1], key[2], 2), "y" + sgn(key[2]), 0.5)
        elif kind in ("AY", "AR2"):
            held.append(((-key[1]) % NY, key[2]) if kind == "AY" else (2, key[1]))
            forward_x()
        elif kind == "XS":
            _, d, zz, s, h = key
            if h == 1 and (zz == 0) == (s > 0):
                send(("XS", d, zz, s, 2), "x" + sgn(s))
            if h == 1:
                under_way[(d, zz)] -= 1
                if not under_way[(d, zz)]:
                    del under_way[(d, zz)]
                    forward_x()

    waited, times = set(), []

    def receive(key):
        program.append(("recv",) + key)
        clock[0] += T_ISSUE
        waited.add(key)
        times.append((clock[0],) + key)

    def passes_on(key):
        if key[0] == "XS":
            return key[4] == 1
        if key[0] == "PY":
            return key[3] == 1
        return key[0] in ("PZ", "AR1", "AR2", "AY")

    for s in (1, -1):
        start_slice(0, s)
        send(("AR1", 0 if s > 0 else 1), "y" + sgn(s))
        send(("XS", 0, 0, s, 1), "x" + sgn(s))
    send(("PC", 0, 0, 0), "c")
    for s in (1, -1):
        send(("XS", 0, 1, s, 1), "x" + sgn(s))
    program.append(("local",))

    jobs = {}
    arrive = {n: {} for n in range(NS)}
    for n in range(NS):
        arrive[n][0] = {("PC", n, 0, 0)}
        for s in (1, -1):
            for h in range(1, FAR + 1):
                for sub in subs(s, h):
                    rel = (-s * h) % NZ
                    arrive[n].setdefault(rel, set()).update({("PZ", n, s, h, sub), ("PC", n, rel, sub + 1 if h == FAR else 0)})
    rows = {}
    for d in range(NY):
        need = {("XS", d, zz, s, 1) for zz in (0, 1) for s in (1, -1)} | {("XS", d, 0, 1, 2), ("XS", d, 1, -1, 2)}
        side = 1 if d == 3 else -1
        rows[d] = need | {0: set(), 2: {("AR2", 0), ("AR2", 1)}}.get(d, {("AY", side, 0), ("AY", side, 1)})
    ready_rows = {("prepA", d) for d in range(NY) if d != LATE_D}
    for d in range(NY):
        if d != LATE_D:
            jobs[("prepA", d)] = (-1.0, rows[d], T_PREP * 8)
    blocks = {("block", 0, zz): {("AY", -1, zz)} for zz in (0, 1)}
    blocks |= {("block", (-s) % NX, zz): {("XS", LATE_D, zz, s, 1)} for zz in (0, 1) for s in (1, -1)}
    blocks |= {("block", 2, 0): {("XS", LATE_D, 0, 1, 2)}, ("block", 2, 1): {("XS", LATE_D, 1, -1, 2)}}
    for job, need in blocks.items():
        jobs[job] = (-1.5, need | {("prepB", n) for n in range(NS) if n not in STEPPED}, T_BLOCK)
    early = {("PY", n, s, h) for n in EARLY for s in (1, -1) for h in (1, 2)}
    for n in range(NS):
        whole = n == NS - 1
        if n in STEPPED:
            steps = {("step", n, rel) for rel in range(NZ)}
            for rel in range(NZ):
                jobs[("step", n, rel)] = (n - 0.5, arrive[n][rel] | ready_rows | (set(blocks) if whole else set()), T_STEP if whole else T_BLOCK)
        else:
            jobs[("prepB", n)] = (-2.0, set().union(*arrive[n].values()), T_PREP * 16)
        done = {}
        for d in range(NY):
            if n not in STEPPED and d == LATE_D:
                done[d] = set(blocks)
            elif n in STEPPED and (whole or d != LATE_D):
                done[d] = steps
            else:
                done[d] = {("task", d, n)}
                need = set(blocks) | steps if n in STEPPED else {("prepA", d), ("prepB", n)}
                jobs[("task", d, n)] = (n + 0.1 * POS[d] - (1 if d == 2 else 0), need, T_TASK)
        everything = set().union(*done.values())
        first = ("vpart", n)
        if n in EARLY:
            jobs[first] = (-3.5, everything | early, 0.15)
        jobs[("y2", n)] = (-3.0, done[2], 0.0)
        for s in (1, -1):
            jobs[("y0", n, s)] = (-2.9, done[s % NY], 0.0)
            jobs[("y1", n, s)] = (-3.0, ({first} if n in EARLY else done[s % NY]) | {("Y2", n, s)}, T_SMALL)
        jobs[("fin", n)] = (-3.0, ({first} if n in EARLY else done[0]) | {("Y1", n, s, i) for s in (1, -1) for i in (0, 1)}, T_SMALL)
    jobs[("vz",)] = (-4.0, {("vpart", n) for n in EARLY} | {("fin", n) for n in range(NS) if n not in EARLY}, 0.0)
    jobs[("vg",)] = (-4.0, {("VZ",)}, 0.05)
    jobs[("vend",)] = (-4.0, {("VG",)}, 0.05)
    while jobs or arrivals:
        if arrivals and arrivals[0][0] <= clock[0]:
            key = heapq.heappop(arrivals)[2]
            got.add(key)
            if passes_on(key):
                receive(key)
                on(key)
            continue
        ready = [(p, j) for j, (p, need, _) in jobs.items() if need <= got]
        if ready:
            job = min(ready, key=lambda r: (r[0], str(r[1])))[1]
            for key in sorted(jobs[job][1], key=str):
                if key[0].isupper() and key not in waited:
                    receive(key)
            program.append(job)
            times.append((clock[0],) + job)
            clock[0] += jobs.pop(job)[2]
            got.add(job)
            if job[0] == "y2":
                for s in (1, -1):
                    send(("Y2", job[1], s), "y" + sgn(s), 0.5)
            elif job[0] == "y1":
                send(("Y1", job[1], job[2], 1), "y" + sgn(job[2]), 0.5)
            elif job[0] == "y0":
                send(("Y1", job[1], job[2], 0), "y" + sgn(job[2]), 0.5)
            elif job[0] in ("vz", "vg"):
                send((job[0].upper(),), job[0])
            continue
        late = sorted((t, k) for k, t in done_at.items() if t + 3.0 < clock[0])
        if late and arrivals and arrivals[0][0] > clock[0] + 0.1:
            program.append(("sent",) + late[0][1])
            del done_at[late[0][1]]
            clock[0] += 0.03
            continue
        clock[0] = max(clock[0], arrivals[0][0])

    final, slots, pool, flying = [], {}, list(range(SEND_POOL)), []
    for act in program:
        key = act[1:]
        if act[0] == "send" and key[0] not in ("VZ", "VG"):
            if not pool:
                old = min(flying, key=lambda k: (ends[k], str(k)))
                final.append(("sent",) + old)
                flying.remove(old)
                pool.append(slots[old])
            slots[key] = pool.pop(0)
            flying.append(key)
        if act[0] == "sent":
            if key not in flying:
                continue
            flying.remove(key)
            pool.append(slots[key])
        final.append(act)
    for key in flying + [("VZ",), ("VG",)]:
        final.append(("sent",) + key)
    return final, slots, clock[0], free, times


def kernel(program, slots, sem_of, pattern_hbm, sigma, panel, cross, var, pattern, pbuf, sbuf, relay, a_hi, a_lo, b_hi, b_lo, part, r1, r2,
           pv, vz, vg, send_sem, recv_sem, local_sem):
    row, x = lax.axis_index("row"), lax.axis_index("col")
    z, y, c = row // (2 * NY), (row // 2) % NY, row % 2
    flip_y = 1 - 2 * c

    def at(dx=0, dy=0, dz=0, flip=False):
        core = 1 - c if flip else c
        return ((((z + dz + NZ) % NZ) * NY + (y + flip_y * dy + NY) % NY) * 2 + core, (x + dx + NX) % NX)

    halves = [pl.ds(0, B // 2), pl.ds(B // 2, B // 2)]

    def lanes(start):
        return pl.ds(pl.multiple_of(start, W), W)

    def ends(key, sender):
        kind = key[0]
        if kind == "PZ":
            _, n, s, h, sub = key
            zs = (z - s * (h - 1 if sender else h) + NZ) % NZ
            dst = pbuf.at[n, 2 * zs + c, halves[sub]]
            src = panel.at[halves[sub], pl.ds(n * W, W)] if h == 1 else dst
            return src, dst, at(dz=s)
        if kind == "PC":
            _, n, rel, part_no = key
            zs = (z + rel) % NZ
            dst = pbuf.at[n, 2 * zs + (c if sender else 1 - c)]
            if part_no:
                dst = pbuf.at[n, 2 * zs + (c if sender else 1 - c), halves[part_no - 1]]
            src = panel.at[:, pl.ds(n * W, W)] if rel == 0 else dst
            return src, dst, at(flip=True)
        if kind == "AY":
            _, s, zz = key
            src = sigma.at[:, lanes(zz * NY * W + ((y + flip_y * s + NY) % NY) * W)]
            return src, sbuf.at[(-s) % NY, 2 * x + zz], at(dy=s)
        if kind == "AR1":
            k = key[1]
            src = sigma.at[:, lanes(k * NY * W + ((y + 2) % NY) * W)]
            return src, relay.at[k], at(dy=1 - 2 * k)
        if kind == "AR2":
            k = key[1]
            return relay.at[k], sbuf.at[2, 2 * x + k], at(dy=1 - 2 * k)
        if kind == "XS":
            _, d, zz, s, h = key
            xs = (x - s * (h - 1 if sender else h) + NX) % NX
            dst = sbuf.at[d, 2 * xs + zz]
            src = sigma.at[:, lanes(zz * NY * W + y * W)] if d == 0 and h == 1 else dst
            return src, dst, at(dx=s)
        if kind == "PY":
            _, n, s, h = key
            e = EARLY.index(n)
            if h == 1:
                return panel.at[:, pl.ds(n * W, W)], pv.at[e, (-s) % NY], at(dy=s)
            half = halves[(1 - s) // 2]
            return pv.at[e, (-s) % NY, half], pv.at[e, 2, half], at(dy=s)
        if kind == "Y2":
            _, n, s = key
            i = 0 if s > 0 else 1
            return part.at[n, POS[2], pl.ds(i * (B // 2), B // 2)], r1.at[i, n], at(dy=s)
        _, n, s, i = key
        half = halves[(1 - s) // 2 if i else (1 + s) // 2]
        return part.at[n, POS[s % NY], half], r2.at[0 if s > 0 else 1, n, half], at(dy=s)

    def copy(key, sender):
        src, dst, target = ends(key, sender)
        return pltpu.make_async_remote_copy(
            src_ref=src if sender else dst, dst_ref=dst, send_sem=send_sem.at[slots[key]], recv_sem=recv_sem.at[sem_of[key]],
            device_id=target, device_id_type=MESH)

    def column_sums(kind, ref=None, peer=None):
        buf, mine = (vz, z) if kind == "VZ" else (vg, me8)
        ref = buf.at[pl.ds(0, 7)] if peer is None else buf.at[mine]
        i = 0 if kind == "VZ" else 1
        return pltpu.make_async_remote_copy(
            src_ref=ref, dst_ref=ref, send_sem=send_sem.at[SEND_POOL + i], recv_sem=recv_sem.at[sem_of[(kind,)]],
            device_id=at(dz=1) if peer is None else peer, device_id_type=MESH)

    me8 = row % (2 * NY)
    barrier = pltpu.get_barrier_semaphore()
    peers = [at(dx=1), at(dx=-1), at(dy=1), at(dy=-1), at(dz=1), at(dz=-1), at(flip=True)]
    for peer in peers:
        pl.semaphore_signal(barrier, inc=1, device_id=peer, device_id_type=MESH)
    locals_ = [pltpu.make_async_copy(panel.at[:, pl.ds(n * W, W)], pbuf.at[n, 2 * z + c], local_sem.at[n]) for n in range(NS)]
    locals_ += [pltpu.make_async_copy(sigma.at[:, lanes(zz * NY * W + y * W)], sbuf.at[0, 2 * x + zz], local_sem.at[NS + zz]) for zz in (0, 1)]
    locals_ += [pltpu.make_async_copy(pattern_hbm, pattern, local_sem.at[NS + 2])]
    pl.semaphore_wait(barrier, len(peers))

    def split_a(d, zk):
        rb = (z * NY + (y + flip_y * d + NY) % NY) * 2 + c
        cb = (zk * NY + y) * 2
        for j in (0, 1):
            m = pattern[rb, cb + j].astype(F32)
            v = sbuf[d, zk, :, pl.ds(j * B, B)] * m
            hi = v.astype(BF16)
            a_hi[zk, pl.ds(POS[d] * B, B), pl.ds(j * B, B)] = hi
            a_lo[zk, pl.ds(POS[d] * B, B), pl.ds(j * B, B)] = (v - hi.astype(F32)).astype(BF16)

    def prep_a(d):
        def one(zk, carry):
            split_a(d, zk)
            return carry

        lax.fori_loop(0, NZ, one, 0)

    def split_b(n, k):
        for j in (0, 1):
            p = pbuf[n, 2 * k + j]
            hi = p.astype(BF16)
            b_hi[n, k, pl.ds(j * B, B)] = hi
            b_lo[n, k, pl.ds(j * B, B)] = (p - hi.astype(F32)).astype(BF16)

    def prep_b(n):
        def one(k, carry):
            split_b(n, k)
            return carry

        lax.fori_loop(0, NZ, one, 0)

    dot = functools.partial(jnp.dot, preferred_element_type=F32)

    def product(n, k, lo, hi):
        ah, al = a_hi[k, pl.ds(lo * B, (hi - lo) * B)], a_lo[k, pl.ds(lo * B, (hi - lo) * B)]
        return dot(ah, b_hi[n, k]) + (dot(ah, b_lo[n, k]) + dot(al, b_hi[n, k]))

    begun = set()

    def add_product(n, k, lo, hi):
        res = product(n, k, lo, hi).reshape(hi - lo, B, W)
        part[n, pl.ds(lo, hi - lo)] = part[n, pl.ds(lo, hi - lo)] + res if (n, lo) in begun else res
        begun.add((n, lo))

    def task(d, n):
        acc = jnp.zeros((B, W), F32)
        for k in range(NZ):
            acc = acc + product(n, k, POS[d], POS[d] + 1)
        part[n, POS[d]] = acc

    def step(n, rel):
        k = (z + rel) % NZ
        split_b(n, k)
        add_product(n, k, 0, NY if n == NS - 1 else NY - 1)

    def block(xr, zz):
        k = 2 * ((x + xr) % NX) + zz
        split_a(LATE_D, k)
        for n in range(NS):
            if n not in STEPPED:
                add_product(n, k, POS[LATE_D], POS[LATE_D] + 1)

    def put_var(n, prod):
        for j in (0, 1):
            vz[z, pl.ds(2 * n + j, 1)] = prod[:, j * B:(j + 1) * B]

    for act in program:
        kind = act[0]
        if kind == "send":
            if act[1] == "VZ":
                for r in range(1, NZ):
                    column_sums("VZ", peer=at(dz=r)).start()
            elif act[1] == "VG":
                for r in range(1, 2 * NY):
                    column_sums("VG", peer=(z * 2 * NY + (me8 + r) % (2 * NY), x)).start()
            else:
                copy(act[1:], True).start()
        elif kind == "recv":
            if act[1] in ("VZ", "VG"):
                column_sums(act[1]).wait_recv()
            else:
                copy(act[1:], False).wait_recv()
        elif kind == "sent":
            if act[1] in ("VZ", "VG"):
                column_sums(act[1]).wait_send()
            else:
                copy(act[1:], True).wait_send()
        elif kind == "local":
            for cp in locals_:
                cp.start()
            for cp in locals_:
                cp.wait()
        elif kind == "prepA":
            prep_a(act[1])
        elif kind == "prepB":
            prep_b(act[1])
        elif kind == "task":
            task(act[1], act[2])
        elif kind == "step":
            step(act[1], act[2])
        elif kind == "block":
            block(act[1], act[2])
        elif kind == "y1":
            _, n, s = act
            i = 0 if s > 0 else 1
            half = pl.ds(i * (B // 2), B // 2)
            part[n, POS[s % NY], half] = part[n, POS[s % NY], half] + r1[i, n]
        elif kind == "fin":
            n = act[1]
            out = part[n, 0] + (r2[0, n] + r2[1, n])
            cross[:, pl.ds(n * W, W)] = out
            if n not in EARLY:
                put_var(n, jnp.sum(out * pbuf[n, 2 * z + c], axis=0, keepdims=True))
        elif kind == "vpart":
            n = act[1]
            prod = part[n, 0] * pbuf[n, 2 * z + c]
            for d in range(1, NY):
                prod = prod + part[n, POS[d]] * pv[EARLY.index(n), d]
            put_var(n, jnp.sum(prod, axis=0, keepdims=True))
        elif kind == "vg":
            total = vz[0]
            for i in range(1, NZ):
                total = total + vz[i]
            vg[me8] = total
        elif kind == "vend":
            total = vg[0]
            for i in range(1, 2 * NY):
                total = total + vg[i]
            var[...] = total


def body(sigma_anc, panel_hat, pattern, diag_inverse):
    program, slots = plan()[:2]
    keys = sorted({act[1:] for act in program if act[0] == "send"}, key=str)
    sem_of = {key: i for i, key in enumerate(keys)}
    dma = pltpu.SemaphoreType.DMA
    vmem = pl.BlockSpec(memory_space=pltpu.VMEM)
    cross, var = pl.pallas_call(
        functools.partial(kernel, program, slots, sem_of),
        out_shape=(pltpu.VMEM((B, NS * W), F32), pltpu.VMEM((8, B), F32)),
        in_specs=[pl.BlockSpec(memory_space=pltpu.HBM)] * 3,
        out_specs=(vmem, vmem),
        scratch_shapes=[
            pltpu.SMEM((NY * NZ * 2, NY * NZ * 2), jnp.int32),
            pltpu.VMEM((NS, 2 * NZ, B, W), F32),
            pltpu.VMEM((NY, NZ, B, W), F32),
            pltpu.VMEM((2, B, W), F32),
            pltpu.VMEM((NZ, NY * B, W), BF16),
            pltpu.VMEM((NZ, NY * B, W), BF16),
            pltpu.VMEM((NS, NZ, W, W), BF16),
            pltpu.VMEM((NS, NZ, W, W), BF16),
            pltpu.VMEM((NS, NY, B, W), F32),
            pltpu.VMEM((2, NS, B // 2, W), F32),
            pltpu.VMEM((2, NS, B, W), F32),
            pltpu.VMEM((len(EARLY), NY, B, W), F32),
            pltpu.VMEM((NZ, 8, B), F32),
            pltpu.VMEM((2 * NY, 8, B), F32),
            dma((SEND_POOL + 2,)),
            dma((len(keys),)),
            dma((NS + 3,)),
        ],
        compiler_params=pltpu.CompilerParams(collective_id=0, has_side_effects=True, vmem_limit_bytes=56 * 1024 * 1024),
        name="selected_inverse",
    )(pattern, sigma_anc, panel_hat)
    return -cross, diag_inverse + var.reshape(-1)


def solution(mesh):
    in_specs = (P("row", "col"), P("row", "col"), P(), P("col"))
    out_specs = (P("row", "col"), P("col"))
    return jax.shard_map(body, mesh=mesh, in_specs=in_specs, out_specs=out_specs, check_vma=False)
```

time: 79.2 us -> 72 us (0.909)
  Pallas kernels: 76.9 us -> 69.8 us
    pallas_call x1, Pallas kernels: 76.9 us -> 69.8 us  [body(): pl.pallas_call(functools.partial(kernel, program, slots, sem_of), out_sha...]
where the time goes in v3:
time: 72 us; the launch traced here: 71.9 us
  Pallas kernels  69.8 us (97%)
  other arithmetic  1.43 us (2%)
    pallas_call x1, Pallas kernels, body(): pl.pallas_call(functools.partial(kernel, program, slots, sem_of), out_sha...  69.8 us

profile of v3, /device:TPU:1, one launch (start us, length us, event | category | flops | bytes accessed | tf_op | source)
XLA Modules:
  0.0 71.9 jit_solution(12133409009310082007)
XLA Ops:
  0.6 69.8 %selected_inverse.1 = (f32[128,1024]{1,0:T(8,128)S(1)}, f32[8,128]{1,0:T(8,128)S(1)}) custom-call(s32[64,64]{1,0:T(8,128)} %pattern_hbm.1, f32[128,2048]{1,0:T(8,128)} %sigma.1, f32[128,1024]{1,0:T(8,128)} %panel.1), custom_call_target="tpu_custom_call" | custom-call | tf_op jit(solution)/shard_map/selected_inverse/pallas_call | solution.py:481
  70.4 0.0 copy-start
  70.5 0.8 %neg.3 = f32[128,1024]{1,0:T(8,128)} negate(f32[128,1024]{1,0:T(8,128)S(1)} %get-tuple-element.4) | non-fusion elementwise | flops 131072 | bytes 1048576 | tf_op jit(solution)/shard_map/neg | solution.py:508
  71.3 0.0 copy-done
  71.3 0.6 bitcast_add_fusion
Async XLA Ops:
  70.4 0.9 %copy-start = (f32[1024]{0:T(1024)S(1)}, f32[1024]{0:T(1024)}, u32[]{:S(2)}) copy-start(f32[1024]{0:T(1024)} %param.7) | copy-start | bytes 12292

commit v4 on v3

--- a/solution.py
+++ b/solution.py
@@ -15,18 +15,19 @@
 NS = 4
 F32, BF16 = jnp.float32, jnp.bfloat16
 
-EARLY = (2, 3)
+EARLY = (0, 1, 2, 3)
 STEPPED = (2, 3)
 LATE_D = 1
 POS = (0, 3, 1, 2)
 FAR = NZ // 2
 SEND_POOL = 40
+FIN = 2.6
 Y_SHARED = 25.0
 X_WINDOW = 2
-NEXT = (None, (1, 2), (2, 3), (1, 2))
-
-LINK, LAT, CORE, CORE_LAT = 2.82, 2.0, 0.3, 1.0
-T_ISSUE, T_PREP, T_TASK, T_SMALL, T_STEP, T_BLOCK = 0.03, 0.035, 0.96, 0.1, 0.5, 0.4
+NEXT = (None, (1, 2), (1, 2), (2, 2))
+
+LINK, LAT, CORE, CORE_LAT = 2.84, 2.1, 0.3, 1.0
+T_ISSUE, T_PREP, T_TASK, T_SMALL, T_STEP, T_PART, T_BLOCK = 0.02, 0.035, 0.97, 0.05, 0.48, 0.36, 0.24
 VZ_LAT, VG_LAT = 4.2, 3.0
 D_ORDER = (0, 2, 3, 1)
 
@@ -50,6 +51,8 @@
         clock[0] += T_ISSUE
         cost, lat = {"c": (CORE, CORE_LAT), "vz": (0.0, VZ_LAT), "vg": (0.0, VG_LAT)}.get(link, (LINK, LAT))
         start = max(clock[0], free.get(link, 0.0))
+        if link == "vg":
+            start = max([start] + [free.get(other, 0.0) for other in ("y+", "y-")])
         took = cost * units
         if link[0] == "y" and clock[0] > Y_SHARED:
             both = min(max(free.get("y+" if link == "y-" else "y-", 0.0) - start, 0.0), took)
@@ -96,16 +99,22 @@
                     if s > 0 and i:
                         send(("PC", n + 1, 0, 0), "c")
         elif kind == "AR1":
-            k = key[1]
+            _, k, sub = key
             y = "y" + "+-"[k]
-            send(("AR2", k), y)
+            send(("AR2", k, sub), y, 0.5)
+            if not sub:
+                return
             for zz in (0, 1):
                 send(("AY", 1 - 2 * k, zz), y)
-            for n in EARLY:
+            for n in EARLY[:2]:
                 send(("PY", n, 1 - 2 * k, 1), y)
         elif kind == "PY" and key[3] == 1:
             send(("PY", key[1], key[2], 2), "y" + sgn(key[2]), 0.5)
+            if EARLY.index(key[1]) + 2 < len(EARLY):
+                send(("PY", EARLY[EARLY.index(key[1]) + 2], key[2], 1), "y" + sgn(key[2]))
         elif kind in ("AY", "AR2"):
+            if kind == "AR2" and not {("AR2", key[1], sub) for sub in (0, 1)} <= waited:
+                return
             held.append(((-key[1]) % NY, key[2]) if kind == "AY" else (2, key[1]))
             forward_x()
         elif kind == "XS":
@@ -135,7 +144,8 @@
 
     for s in (1, -1):
         start_slice(0, s)
-        send(("AR1", 0 if s > 0 else 1), "y" + sgn(s))
+        for sub in (0, 1):
+            send(("AR1", 0 if s > 0 else 1, sub), "y" + sgn(s), 0.5)
         send(("XS", 0, 0, s, 1), "x" + sgn(s))
     send(("PC", 0, 0, 0), "c")
     for s in (1, -1):
@@ -155,7 +165,7 @@
     for d in range(NY):
         need = {("XS", d, zz, s, 1) for zz in (0, 1) for s in (1, -1)} | {("XS", d, 0, 1, 2), ("XS", d, 1, -1, 2)}
         side = 1 if d == 3 else -1
-        rows[d] = need | {0: set(), 2: {("AR2", 0), ("AR2", 1)}}.get(d, {("AY", side, 0), ("AY", side, 1)})
+        rows[d] = need | {0: set(), 2: {("AR2", k, sub) for k in (0, 1) for sub in (0, 1)}}.get(d, {("AY", side, 0), ("AY", side, 1)})
     ready_rows = {("prepA", d) for d in range(NY) if d != LATE_D}
     for d in range(NY):
         if d != LATE_D:
@@ -165,13 +175,12 @@
     blocks |= {("block", 2, 0): {("XS", LATE_D, 0, 1, 2)}, ("block", 2, 1): {("XS", LATE_D, 1, -1, 2)}}
     for job, need in blocks.items():
         jobs[job] = (-1.5, need | {("prepB", n) for n in range(NS) if n not in STEPPED}, T_BLOCK)
-    early = {("PY", n, s, h) for n in EARLY for s in (1, -1) for h in (1, 2)}
     for n in range(NS):
         whole = n == NS - 1
         if n in STEPPED:
             steps = {("step", n, rel) for rel in range(NZ)}
             for rel in range(NZ):
-                jobs[("step", n, rel)] = (n - 0.5, arrive[n][rel] | ready_rows | (set(blocks) if whole else set()), T_STEP if whole else T_BLOCK)
+                jobs[("step", n, rel)] = (n - 0.5, arrive[n][rel] | ready_rows | (set(blocks) if whole else set()), T_STEP if whole else T_PART)
         else:
             jobs[("prepB", n)] = (-2.0, set().union(*arrive[n].values()), T_PREP * 16)
         done = {}
@@ -187,15 +196,15 @@
         everything = set().union(*done.values())
         first = ("vpart", n)
         if n in EARLY:
-            jobs[first] = (-3.5, everything | early, 0.15)
+            jobs[first] = (-3.5, everything | {("PY", n, s, h) for s in (1, -1) for h in (1, 2)}, 0.1)
         jobs[("y2", n)] = (-3.0, done[2], 0.0)
         for s in (1, -1):
             jobs[("y0", n, s)] = (-2.9, done[s % NY], 0.0)
-            jobs[("y1", n, s)] = (-3.0, ({first} if n in EARLY else done[s % NY]) | {("Y2", n, s)}, T_SMALL)
-        jobs[("fin", n)] = (-3.0, ({first} if n in EARLY else done[0]) | {("Y1", n, s, i) for s in (1, -1) for i in (0, 1)}, T_SMALL)
-    jobs[("vz",)] = (-4.0, {("vpart", n) for n in EARLY} | {("fin", n) for n in range(NS) if n not in EARLY}, 0.0)
-    jobs[("vg",)] = (-4.0, {("VZ",)}, 0.05)
-    jobs[("vend",)] = (-4.0, {("VG",)}, 0.05)
+            jobs[("y1", n, s)] = (-3.0, done[s % NY] | {("Y2", n, s)}, T_SMALL)
+        jobs[("fin", n)] = (FIN, ({first} if n in EARLY else done[0]) | {("Y1", n, s, i) for s in (1, -1) for i in (0, 1)}, T_SMALL)
+    jobs[("v1",)] = (-4.0, {("vpart", n) for n in EARLY} | {("fin", n) for n in range(NS) if n not in EARLY}, 0.0)
+    jobs[("v2",)] = (-4.0, {("VG",)}, 0.05)
+    jobs[("vend",)] = (-4.0, {("VZ",)}, 0.05)
     while jobs or arrivals:
         if arrivals and arrivals[0][0] <= clock[0]:
             key = heapq.heappop(arrivals)[2]
@@ -221,8 +230,10 @@
                 send(("Y1", job[1], job[2], 1), "y" + sgn(job[2]), 0.5)
             elif job[0] == "y0":
                 send(("Y1", job[1], job[2], 0), "y" + sgn(job[2]), 0.5)
-            elif job[0] in ("vz", "vg"):
-                send((job[0].upper(),), job[0])
+            elif job[0] == "v1":
+                send(("VG",), "vg")
+            elif job[0] == "v2":
+                send(("VZ",), "vz")
             continue
         late = sorted((t, k) for k, t in done_at.items() if t + 3.0 < clock[0])
         if late and arrivals and arrivals[0][0] > clock[0] + 0.1:
@@ -254,7 +265,41 @@
     return final, slots, clock[0], free, times
 
 
-def kernel(program, slots, sem_of, pattern_hbm, sigma, panel, cross, var, pattern, pbuf, sbuf, relay, a_hi, a_lo, b_hi, b_lo, part, r1, r2,
+def receive_slots(program):
+    at = {act: i for i, act in enumerate(program)}
+    keys = [act[1:] for act in program if act[0] == "send"]
+
+    def channel(key):
+        if key[0] == "PC":
+            return "c", 0
+        if key[0] in ("AR1", "AR2"):
+            return "y", 1 - 2 * key[1]
+        return {"P": "z", "X": "x", "A": "y", "Y": "y"}["Y" if key[0] == "PY" else key[0][0]], key[{"PZ": 2, "XS": 3, "AY": 1, "PY": 2, "Y2": 2, "Y1": 2}[key[0]]]
+
+    slots, users = {}, []
+    for key in keys:
+        if key[0] in ("VZ", "VG"):
+            users.append(None)
+            slots[key] = len(users) - 1
+            continue
+        axis, s = channel(key)
+        back = [m for m in keys if m[0] not in ("VZ", "VG") and channel(m) == (axis, -s)]
+        free = None
+        for i, last in enumerate(users):
+            if last is None or channel(last) != (axis, s):
+                continue
+            if any(at[("send",) + m] > at[("recv",) + last] and at[("recv",) + m] < at[("send",) + key] for m in back):
+                free = i
+                break
+        if free is None:
+            users.append(key)
+            free = len(users) - 1
+        users[free] = key
+        slots[key] = free
+    return slots
+
+
+def kernel(program, slots, sem_of, pattern_hbm, sigma, panel, diag_hbm, cross, var, diag, pattern, pbuf, sbuf, relay, a_hi, a_lo, b_hi, b_lo, part, r1, r2,
            pv, vz, vg, send_sem, recv_sem, local_sem):
     row, x = lax.axis_index("row"), lax.axis_index("col")
     z, y, c = row // (2 * NY), (row // 2) % NY, row % 2
@@ -290,12 +335,12 @@
             src = sigma.at[:, lanes(zz * NY * W + ((y + flip_y * s + NY) % NY) * W)]
             return src, sbuf.at[(-s) % NY, 2 * x + zz], at(dy=s)
         if kind == "AR1":
-            k = key[1]
-            src = sigma.at[:, lanes(k * NY * W + ((y + 2) % NY) * W)]
-            return src, relay.at[k], at(dy=1 - 2 * k)
+            _, k, sub = key
+            src = sigma.at[halves[sub], lanes(k * NY * W + ((y + 2) % NY) * W)]
+            return src, relay.at[k, halves[sub]], at(dy=1 - 2 * k)
         if kind == "AR2":
-            k = key[1]
-            return relay.at[k], sbuf.at[2, 2 * x + k], at(dy=1 - 2 * k)
+            _, k, sub = key
+            return relay.at[k, halves[sub]], sbuf.at[2, 2 * x + k, halves[sub]], at(dy=1 - 2 * k)
         if kind == "XS":
             _, d, zz, s, h = key
             xs = (x - s * (h - 1 if sender else h) + NX) % NX
@@ -315,7 +360,8 @@
             return part.at[n, POS[2], pl.ds(i * (B // 2), B // 2)], r1.at[i, n], at(dy=s)
         _, n, s, i = key
         half = halves[(1 - s) // 2 if i else (1 + s) // 2]
-        return part.at[n, POS[s % NY], half], r2.at[0 if s > 0 else 1, n, half], at(dy=s)
+        side = 0 if s > 0 else 1
+        return r1.at[side, n] if i else part.at[n, POS[s % NY], half], r2.at[0 if s > 0 else 1, n, half], at(dy=s)
 
     def copy(key, sender):
         src, dst, target = ends(key, sender)
@@ -339,6 +385,7 @@
     locals_ = [pltpu.make_async_copy(panel.at[:, pl.ds(n * W, W)], pbuf.at[n, 2 * z + c], local_sem.at[n]) for n in range(NS)]
     locals_ += [pltpu.make_async_copy(sigma.at[:, lanes(zz * NY * W + y * W)], sbuf.at[0, 2 * x + zz], local_sem.at[NS + zz]) for zz in (0, 1)]
     locals_ += [pltpu.make_async_copy(pattern_hbm, pattern, local_sem.at[NS + 2])]
+    locals_ += [pltpu.make_async_copy(diag_hbm, diag, local_sem.at[NS + 3])]
     pl.semaphore_wait(barrier, len(peers))
 
     def split_a(d, zk):
@@ -405,7 +452,7 @@
 
     def put_var(n, prod):
         for j in (0, 1):
-            vz[z, pl.ds(2 * n + j, 1)] = prod[:, j * B:(j + 1) * B]
+            vg[me8, pl.ds(2 * n + j, 1)] = prod[:, j * B:(j + 1) * B]
 
     for act in program:
         kind = act[0]
@@ -447,11 +494,11 @@
             _, n, s = act
             i = 0 if s > 0 else 1
             half = pl.ds(i * (B // 2), B // 2)
-            part[n, POS[s % NY], half] = part[n, POS[s % NY], half] + r1[i, n]
+            r1[i, n] = part[n, POS[s % NY], half] + r1[i, n]
         elif kind == "fin":
             n = act[1]
             out = part[n, 0] + (r2[0, n] + r2[1, n])
-            cross[:, pl.ds(n * W, W)] = out
+            cross[:, pl.ds(n * W, W)] = -out
             if n not in EARLY:
                 put_var(n, jnp.sum(out * pbuf[n, 2 * z + c], axis=0, keepdims=True))
         elif kind == "vpart":
@@ -460,30 +507,38 @@
             for d in range(1, NY):
                 prod = prod + part[n, POS[d]] * pv[EARLY.index(n), d]
             put_var(n, jnp.sum(prod, axis=0, keepdims=True))
-        elif kind == "vg":
+        elif kind == "v2":
+            total = vg[0]
+            for i in range(1, 2 * NY):
+                total = total + vg[i]
+            vz[z] = total
+        elif kind == "vend":
             total = vz[0]
             for i in range(1, NZ):
                 total = total + vz[i]
-            vg[me8] = total
-        elif kind == "vend":
-            total = vg[0]
-            for i in range(1, 2 * NY):
-                total = total + vg[i]
-            var[...] = total
+            var[...] = diag[...] + total
+
+
+def finish(cross, var, cross_out, var_out, sem):
+    copies = [pltpu.make_async_copy(cross, cross_out, sem.at[0]), pltpu.make_async_copy(var, var_out, sem.at[1])]
+    for copy in copies:
+        copy.start()
+    for copy in copies:
+        copy.wait()
 
 
 def body(sigma_anc, panel_hat, pattern, diag_inverse):
     program, slots = plan()[:2]
-    keys = sorted({act[1:] for act in program if act[0] == "send"}, key=str)
-    sem_of = {key: i for i, key in enumerate(keys)}
+    sem_of = receive_slots(program)
     dma = pltpu.SemaphoreType.DMA
     vmem = pl.BlockSpec(memory_space=pltpu.VMEM)
     cross, var = pl.pallas_call(
         functools.partial(kernel, program, slots, sem_of),
         out_shape=(pltpu.VMEM((B, NS * W), F32), pltpu.VMEM((8, B), F32)),
-        in_specs=[pl.BlockSpec(memory_space=pltpu.HBM)] * 3,
+        in_specs=[pl.BlockSpec(memory_space=pltpu.HBM)] * 4,
         out_specs=(vmem, vmem),
         scratch_shapes=[
+            pltpu.VMEM((8, B), F32),
             pltpu.SMEM((NY * NZ * 2, NY * NZ * 2), jnp.int32),
             pltpu.VMEM((NS, 2 * NZ, B, W), F32),
             pltpu.VMEM((NY, NZ, B, W), F32),
@@ -499,13 +554,21 @@
             pltpu.VMEM((NZ, 8, B), F32),
             pltpu.VMEM((2 * NY, 8, B), F32),
             dma((SEND_POOL + 2,)),
-            dma((len(keys),)),
-            dma((NS + 3,)),
+            dma((max(sem_of.values()) + 1,)),
+            dma((NS + 4,)),
         ],
         compiler_params=pltpu.CompilerParams(collective_id=0, has_side_effects=True, vmem_limit_bytes=56 * 1024 * 1024),
         name="selected_inverse",
-    )(pattern, sigma_anc, panel_hat)
-    return -cross, diag_inverse + var.reshape(-1)
+    )(pattern, sigma_anc, panel_hat, diag_inverse.reshape(8, B))
+    out, var = pl.pallas_call(
+        finish,
+        out_shape=(jax.ShapeDtypeStruct((B, NS * W), F32), jax.ShapeDtypeStruct((8, B), F32)),
+        in_specs=[vmem, vmem],
+        out_specs=(pl.BlockSpec(memory_space=pl.ANY),) * 2,
+        scratch_shapes=[dma((2,))],
+        name="finish",
+    )(pltpu.with_memory_space_constraint(cross, pltpu.VMEM), pltpu.with_memory_space_constraint(var, pltpu.VMEM))
+    return out, var.reshape(-1)
 
 
 def solution(mesh):

time: 72 us -> 67.9 us (0.943)
  Pallas kernels: 69.8 us -> 66.8 us
  other arithmetic: 1.43 us -> 0 us
    pallas_call x1, Pallas kernels: 69.8 us -> 66 us  [body(): pl.pallas_call(functools.partial(kernel, program, slots, sem_of), out_sha...]
    neg x1 -> x0, other arithmetic: 0.84 us -> none  [body(): return (-cross, diag_inverse + var.reshape(-1))]
    pallas_call x0 -> x1, Pallas kernels: none -> 0.81 us  [body(): pl.pallas_call(finish, out_shape=(jax.ShapeDtypeStruct((B, NS * W), F32),...]
where the time goes in v4:
time: 67.9 us; the launch traced here: 67.5 us
  Pallas kernels  66.8 us (98%)
    pallas_call x1, Pallas kernels, body(): pl.pallas_call(functools.partial(kernel, program, slots, sem_of), out_sha...  66 us

profile of v4, /device:TPU:1, one launch (start us, length us, event | category | flops | bytes accessed | tf_op | source)
XLA Modules:
  0.0 67.5 jit_solution(3278853031222523757)
XLA Ops:
  0.6 66.0 %selected_inverse.1 = (f32[128,1024]{1,0:T(8,128)S(1)}, f32[8,128]{1,0:T(8,128)S(1)}) custom-call(s32[64,64]{1,0:T(8,128)} %pattern_hbm.1, f32[128,2048]{1,0:T(8,128)} %sigma.1, f32[128,1024]{1,0:T(8,128)} %panel.1, f32[8,128]{1,0:T(8,128)} %bitcast.2), custom_call_target="tpu_custom_call" | custom-call | tf_op jit(solution)/shard_map/selected_inverse/pallas_call | solution.py:535
  66.7 0.8 %finish.1 = (f32[128,1024]{1,0:T(8,128)}, f32[8,128]{1,0:T(8,128)}) custom-call(f32[128,1024]{1,0:T(8,128)S(1)} %get-tuple-element.6.cross, f32[8,128]{1,0:T(8,128)S(1)} %get-tuple-element.7.var), custom_call_target="tpu_custom_call" | custom-call | tf_op jit(solution)/shard_map/finish/pallas_call | solution.py:563

commit v5 on v4

--- a/solution.py
+++ b/solution.py
@@ -22,9 +22,12 @@
 FAR = NZ // 2
 SEND_POOL = 40
 FIN = 2.6
+Y_EXTRA = 0.4
+AHEAD = 2
+Y0 = -2.9
 Y_SHARED = 25.0
 X_WINDOW = 2
-NEXT = (None, (1, 2), (1, 2), (2, 2))
+NEXT = (None, (1, 1), (2, 2), (1, 2))
 
 LINK, LAT, CORE, CORE_LAT = 2.84, 2.1, 0.3, 1.0
 T_ISSUE, T_PREP, T_TASK, T_SMALL, T_STEP, T_PART, T_BLOCK = 0.02, 0.035, 0.97, 0.05, 0.48, 0.36, 0.24
@@ -56,11 +59,12 @@
         took = cost * units
         if link[0] == "y" and clock[0] > Y_SHARED:
             both = min(max(free.get("y+" if link == "y-" else "y-", 0.0) - start, 0.0), took)
+            both = took if key[0] == "Y2" else both
             took = (took + both) / 2
         free[link] = start + took
         done_at[key] = ends[key] = free[link]
         seq[0] += 1
-        heapq.heappush(arrivals, (free[link] + lat, seq[0], key))
+        heapq.heappush(arrivals, (free[link] + lat + (Y_EXTRA if key[0] in ("Y1", "Y2") else 0.0), seq[0], key))
 
     def pz(n, s, h, sub):
         send(("PZ", n, s, h, sub), "z" + sgn(s), 0.5)
@@ -119,15 +123,15 @@
             forward_x()
         elif kind == "XS":
             _, d, zz, s, h = key
-            if h == 1 and (zz == 0) == (s > 0):
-                send(("XS", d, zz, s, 2), "x" + sgn(s))
+            if h == 1:
+                send(("XS", d, zz, s, 2), "x" + sgn(s), 0.5)
             if h == 1:
                 under_way[(d, zz)] -= 1
                 if not under_way[(d, zz)]:
                     del under_way[(d, zz)]
                     forward_x()
 
-    waited, times = set(), []
+    waited, times, came = set(), [], {}
 
     def receive(key):
         program.append(("recv",) + key)
@@ -163,7 +167,7 @@
                     arrive[n].setdefault(rel, set()).update({("PZ", n, s, h, sub), ("PC", n, rel, sub + 1 if h == FAR else 0)})
     rows = {}
     for d in range(NY):
-        need = {("XS", d, zz, s, 1) for zz in (0, 1) for s in (1, -1)} | {("XS", d, 0, 1, 2), ("XS", d, 1, -1, 2)}
+        need = {("XS", d, zz, s, h) for zz in (0, 1) for s in (1, -1) for h in (1, 2)}
         side = 1 if d == 3 else -1
         rows[d] = need | {0: set(), 2: {("AR2", k, sub) for k in (0, 1) for sub in (0, 1)}}.get(d, {("AY", side, 0), ("AY", side, 1)})
     ready_rows = {("prepA", d) for d in range(NY) if d != LATE_D}
@@ -172,7 +176,7 @@
             jobs[("prepA", d)] = (-1.0, rows[d], T_PREP * 8)
     blocks = {("block", 0, zz): {("AY", -1, zz)} for zz in (0, 1)}
     blocks |= {("block", (-s) % NX, zz): {("XS", LATE_D, zz, s, 1)} for zz in (0, 1) for s in (1, -1)}
-    blocks |= {("block", 2, 0): {("XS", LATE_D, 0, 1, 2)}, ("block", 2, 1): {("XS", LATE_D, 1, -1, 2)}}
+    blocks |= {("block", 2, zz): {("XS", LATE_D, zz, s, 2) for s in (1, -1)} for zz in (0, 1)}
     for job, need in blocks.items():
         jobs[job] = (-1.5, need | {("prepB", n) for n in range(NS) if n not in STEPPED}, T_BLOCK)
     for n in range(NS):
@@ -199,15 +203,17 @@
             jobs[first] = (-3.5, everything | {("PY", n, s, h) for s in (1, -1) for h in (1, 2)}, 0.1)
         jobs[("y2", n)] = (-3.0, done[2], 0.0)
         for s in (1, -1):
-            jobs[("y0", n, s)] = (-2.9, done[s % NY], 0.0)
-            jobs[("y1", n, s)] = (-3.0, done[s % NY] | {("Y2", n, s)}, T_SMALL)
+            after = {("y2", AHEAD)} if s % NY == LATE_D and n < AHEAD and n not in STEPPED else set()
+            jobs[("y0", n, s)] = (Y0, done[s % NY] | after, 0.0)
+            jobs[("y1", n, s)] = (-3.0, done[s % NY] | {("Y2", n, s)} | after, T_SMALL)
         jobs[("fin", n)] = (FIN, ({first} if n in EARLY else done[0]) | {("Y1", n, s, i) for s in (1, -1) for i in (0, 1)}, T_SMALL)
     jobs[("v1",)] = (-4.0, {("vpart", n) for n in EARLY} | {("fin", n) for n in range(NS) if n not in EARLY}, 0.0)
     jobs[("v2",)] = (-4.0, {("VG",)}, 0.05)
     jobs[("vend",)] = (-4.0, {("VZ",)}, 0.05)
     while jobs or arrivals:
         if arrivals and arrivals[0][0] <= clock[0]:
-            key = heapq.heappop(arrivals)[2]
+            when, _, key = heapq.heappop(arrivals)
+            came[key] = when
             got.add(key)
             if passes_on(key):
                 receive(key)
@@ -234,6 +240,10 @@
                 send(("VG",), "vg")
             elif job[0] == "v2":
                 send(("VZ",), "vz")
+            continue
+        old = [k for k in came if k not in waited and k[0] != "Y1" and came[k] + 2.0 < clock[0]]
+        if old and arrivals and arrivals[0][0] > clock[0] + 0.1:
+            receive(min(old, key=lambda k: (came[k], str(k))))
             continue
         late = sorted((t, k) for k, t in done_at.items() if t + 3.0 < clock[0])
         if late and arrivals and arrivals[0][0] > clock[0] + 0.1:
@@ -345,6 +355,8 @@
             _, d, zz, s, h = key
             xs = (x - s * (h - 1 if sender else h) + NX) % NX
             dst = sbuf.at[d, 2 * xs + zz]
+            if h == 2:
+                dst = sbuf.at[d, 2 * xs + zz, halves[(1 - s) // 2]]
             src = sigma.at[:, lanes(zz * NY * W + y * W)] if d == 0 and h == 1 else dst
             return src, dst, at(dx=s)
         if kind == "PY":

time: 67.9 us -> 66.3 us (0.976)
  Pallas kernels: 66.8 us -> 65.5 us
    pallas_call x1, Pallas kernels: 66 us -> 64.7 us  [body(): pl.pallas_call(functools.partial(kernel, program, slots, sem_of), out_sha...]
where the time goes in v5:
time: 66.3 us; the launch traced here: 66.1 us
  Pallas kernels  65.5 us (99%)
    pallas_call x1, Pallas kernels, body(): pl.pallas_call(functools.partial(kernel, program, slots, sem_of), out_sha...  64.7 us

profile of v5, /device:TPU:1, one launch (start us, length us, event | category | flops | bytes accessed | tf_op | source)
XLA Modules:
  0.0 66.1 jit_solution(12750753893191895196)
XLA Ops:
  0.6 64.7 %selected_inverse.1 = (f32[128,1024]{1,0:T(8,128)S(1)}, f32[8,128]{1,0:T(8,128)S(1)}) custom-call(s32[64,64]{1,0:T(8,128)} %pattern_hbm.1, f32[128,2048]{1,0:T(8,128)} %sigma.1, f32[128,1024]{1,0:T(8,128)} %panel.1, f32[8,128]{1,0:T(8,128)} %bitcast.2), custom_call_target="tpu_custom_call" | custom-call | tf_op jit(solution)/shard_map/selected_inverse/pallas_call | solution.py:547
  65.3 0.8 %finish.1 = (f32[128,1024]{1,0:T(8,128)}, f32[8,128]{1,0:T(8,128)}) custom-call(f32[128,1024]{1,0:T(8,128)S(1)} %get-tuple-element.6.cross, f32[8,128]{1,0:T(8,128)S(1)} %get-tuple-element.7.var), custom_call_target="tpu_custom_call" | custom-call | tf_op jit(solution)/shard_map/finish/pallas_call | solution.py:575

commit v6 on v5

--- a/solution.py
+++ b/solution.py
@@ -16,14 +16,15 @@
 F32, BF16 = jnp.float32, jnp.bfloat16
 
 EARLY = (0, 1, 2, 3)
+LAST = NS - 1
 STEPPED = (2, 3)
 LATE_D = 1
 POS = (0, 3, 1, 2)
 FAR = NZ // 2
-SEND_POOL = 40
+SEND_POOL = 24
 FIN = 2.6
 Y_EXTRA = 0.4
-AHEAD = 2
+AHEAD = 0
 Y0 = -2.9
 Y_SHARED = 25.0
 X_WINDOW = 2
@@ -206,7 +207,7 @@
             after = {("y2", AHEAD)} if s % NY == LATE_D and n < AHEAD and n not in STEPPED else set()
             jobs[("y0", n, s)] = (Y0, done[s % NY] | after, 0.0)
             jobs[("y1", n, s)] = (-3.0, done[s % NY] | {("Y2", n, s)} | after, T_SMALL)
-        jobs[("fin", n)] = (FIN, ({first} if n in EARLY else done[0]) | {("Y1", n, s, i) for s in (1, -1) for i in (0, 1)}, T_SMALL)
+        jobs[("fin", n)] = (FIN, ({first} if n in EARLY else done[0]) | {("Y1", n, s, i) for s in (1, -1) for i in (0, 1)} | {("vpart", LAST)}, T_SMALL)
     jobs[("v1",)] = (-4.0, {("vpart", n) for n in EARLY} | {("fin", n) for n in range(NS) if n not in EARLY}, 0.0)
     jobs[("v2",)] = (-4.0, {("VG",)}, 0.05)
     jobs[("vend",)] = (-4.0, {("VZ",)}, 0.05)
@@ -296,7 +297,7 @@
         back = [m for m in keys if m[0] not in ("VZ", "VG") and channel(m) == (axis, -s)]
         free = None
         for i, last in enumerate(users):
-            if last is None or channel(last) != (axis, s):
+            if last is None:
                 continue
             if any(at[("send",) + m] > at[("recv",) + last] and at[("recv",) + m] < at[("send",) + key] for m in back):
                 free = i

time: 66.3 us -> 65.7 us (level)
  no operation moved by 1% of the time
where the time goes in v6:
time: 65.7 us; the launch traced here: 65.6 us
  Pallas kernels  65 us (99%)
    pallas_call x1, Pallas kernels, body(): pl.pallas_call(functools.partial(kernel, program, slots, sem_of), out_sha...  64.2 us

profile of v6, /device:TPU:1, one launch (start us, length us, event | category | flops | bytes accessed | tf_op | source)
XLA Modules:
  0.0 65.6 jit_solution(7203895734523371640)
XLA Ops:
  0.6 64.2 %selected_inverse.1 = (f32[128,1024]{1,0:T(8,128)S(1)}, f32[8,128]{1,0:T(8,128)S(1)}) custom-call(s32[64,64]{1,0:T(8,128)} %pattern_hbm.1, f32[128,2048]{1,0:T(8,128)} %sigma.1, f32[128,1024]{1,0:T(8,128)} %panel.1, f32[8,128]{1,0:T(8,128)} %bitcast.2), custom_call_target="tpu_custom_call" | custom-call | tf_op jit(solution)/shard_map/selected_inverse/pallas_call | solution.py:548
  64.8 0.8 %finish.1 = (f32[128,1024]{1,0:T(8,128)}, f32[8,128]{1,0:T(8,128)}) custom-call(f32[128,1024]{1,0:T(8,128)S(1)} %get-tuple-element.6.cross, f32[8,128]{1,0:T(8,128)S(1)} %get-tuple-element.7.var), custom_call_target="tpu_custom_call" | custom-call | tf_op jit(solution)/shard_map/finish/pallas_call | solution.py:576

commit v7 on v6

--- a/solution.py
+++ b/solution.py
@@ -21,14 +21,14 @@
 LATE_D = 1
 POS = (0, 3, 1, 2)
 FAR = NZ // 2
-SEND_POOL = 24
+SEND_POOL = 32
 FIN = 2.6
 Y_EXTRA = 0.4
 AHEAD = 0
 Y0 = -2.9
 Y_SHARED = 25.0
 X_WINDOW = 2
-NEXT = (None, (1, 1), (2, 2), (1, 2))
+NEXT = (None, (0, 1), (1, 3), (2, 3))
 
 LINK, LAT, CORE, CORE_LAT = 2.84, 2.1, 0.3, 1.0
 T_ISSUE, T_PREP, T_TASK, T_SMALL, T_STEP, T_PART, T_BLOCK = 0.02, 0.035, 0.97, 0.05, 0.48, 0.36, 0.24
@@ -155,6 +155,9 @@
     send(("PC", 0, 0, 0), "c")
     for s in (1, -1):
         send(("XS", 0, 1, s, 1), "x" + sgn(s))
+        for i, after in enumerate(NEXT[1]):
+            if not after:
+                pz(1, s, 1, subs(s, 1)[i])
     program.append(("local",))
 
     jobs = {}

time: 65.7 us -> 66.5 us (1.012)
  Pallas kernels: 65 us -> 65.7 us
    pallas_call x1, Pallas kernels: 64.2 us -> 64.9 us  [body(): pl.pallas_call(functools.partial(kernel, program, slots, sem_of), out_sha...]
where the time goes in v7:
time: 66.5 us; the launch traced here: 66.4 us
  Pallas kernels  65.7 us (99%)
    pallas_call x1, Pallas kernels, body(): pl.pallas_call(functools.partial(kernel, program, slots, sem_of), out_sha...  64.9 us

profile of v7, /device:TPU:1, one launch (start us, length us, event | category | flops | bytes accessed | tf_op | source)
XLA Modules:
  0.0 66.4 jit_solution(17201892459184222731)
XLA Ops:
  0.6 64.9 %selected_inverse.1 = (f32[128,1024]{1,0:T(8,128)S(1)}, f32[8,128]{1,0:T(8,128)S(1)}) custom-call(s32[64,64]{1,0:T(8,128)} %pattern_hbm.1, f32[128,2048]{1,0:T(8,128)} %sigma.1, f32[128,1024]{1,0:T(8,128)} %panel.1, f32[8,128]{1,0:T(8,128)} %bitcast.2), custom_call_target="tpu_custom_call" | custom-call | tf_op jit(solution)/shard_map/selected_inverse/pallas_call | solution.py:551
  65.5 0.8 %finish.1 = (f32[128,1024]{1,0:T(8,128)}, f32[8,128]{1,0:T(8,128)}) custom-call(f32[128,1024]{1,0:T(8,128)S(1)} %get-tuple-element.6.cross, f32[8,128]{1,0:T(8,128)S(1)} %get-tuple-element.7.var), custom_call_target="tpu_custom_call" | custom-call | tf_op jit(solution)/shard_map/finish/pallas_call | solution.py:579
